TPU v7x, 128 devices: a whole 4x4x4 slice. The times are simulated.
128 devices in a mesh: grp: 4 (over z_hi, core), dev: 32 (over y, x, z_lo).
Axes of the slice: x: 4, y: 4, z: 4 (z_hi: 2, z_lo: 2; z = z_hi * 2 + z_lo), core: 2. Of those that a mesh axis runs over, the one named last changes fastest.
Arguments:
- layer_input: bfloat16 [262144, 1024], P(('grp', 'dev')), may hold values from -24 to 24
- hidden_pre: bfloat16 [262144, 1024], P(('grp', 'dev')), may hold values from -24 to 24
- out_grad: bfloat16 [262144, 512], P(('grp', 'dev')), may hold values from -6 to 6
- second_weight: bfloat16 [1024, 512], replicated, may hold values from -0.25 to 0.25
- row_grads: bfloat16 [262144, 128], P(('grp', 'dev')), may hold values from -6 to 6
- row_ids: int32 [262144], P(('grp', 'dev')), may hold values from 0 to 2047
- block_counts: int32 [4096], P(('grp', 'dev')), may hold values from 1 to 64, as said below
- emb_table: float32 [65536, 128], P('dev'), may hold values from -4 to 4
- adagrad_state: float32 [65536, 128], P('dev'), may hold values from 0.01 to 1
Outputs:
- grad_first: float32 [1024, 1024], P(('grp', 'dev'))
- grad_second: float32 [1024, 512], P(('grp', 'dev'))
- new_table: float32 [65536, 128], P('dev')
- new_state: float32 [65536, 128], P('dev')
Inputs may be any that keep to these rules, and one draw needn't show every extreme that they name: `block_counts`: the used slots of a block are its first ones. In every draw some owner receives full blocks of 64 used slots from every device. `row_ids`: only used slots are read.
All inputs are finite; a program needn't handle non-finite values.
Results may differ from a plain program's by a relative error of at most 0.0029.
Values may be sent and summed in bfloat16 or wider, within the bound.
No kernel may reach another device: no remote copies, remote signals or barrier semaphores. Data moves between devices by JAX's collectives and lax.ppermute only.
A program may use at most 128 MiB of HBM per device.

v0:
```python
import jax
import jax.numpy as jnp
from jax import lax
from jax.sharding import PartitionSpec as P

learn_rate = 0.5
epsilon = 1e-08


def split_up(array, dim, devices):
    before, after = (array.shape[:dim], array.shape[dim + 1 :])
    return jnp.moveaxis(array.reshape(*before, devices, -1, *after), dim, 0)


def summed_on_arrival(array, axis, dim):
    devices = lax.axis_size(axis)
    blocks = lax.all_to_all(split_up(array, dim, devices), axis, 0, 0, tiled=True)
    return jnp.sum(blocks, axis=0)


def segment_rows(gathered, targets, owned):
    height = 512

    def one_block(index):
        wanted = index * height + jnp.arange(height, dtype=jnp.int32)
        onehot = (wanted[:, None] == targets[None, :]).astype(jnp.bfloat16)
        return jnp.dot(onehot, gathered, preferred_element_type=jnp.float32)

    result = lax.map(one_block, jnp.arange(owned // height, dtype=jnp.int32))
    return result.reshape(owned, gathered.shape[1])


def on_device(
    layer_input,
    hidden_pre,
    out_grad,
    second_weight,
    row_grads,
    row_ids,
    block_counts,
    emb_table,
    adagrad_state,
):
    active = jnp.maximum(hidden_pre, jnp.zeros_like(hidden_pre))
    back = jnp.dot(out_grad, second_weight.T, preferred_element_type=jnp.float32)
    d_hidden = (back * (hidden_pre > 0).astype(jnp.float32)).astype(jnp.bfloat16)
    contract = (((0,), (0,)), ((), ()))
    owners = lax.axis_size("dev")
    capacity = row_grads.shape[0] // owners
    usable = (jnp.arange(capacity, dtype=jnp.int32)[None, :] < block_counts[:, None]).reshape(-1)
    sent_ids = jnp.where(usable, row_ids, -1)
    got_grads, got_ids = (
        lax.all_to_all(row_grads, "dev", split_axis=0, concat_axis=0, tiled=True),
        lax.all_to_all(sent_ids, "dev", split_axis=0, concat_axis=0, tiled=True),
    )
    columns = layer_input
    first_share = summed_on_arrival(
        lax.dot_general(columns, d_hidden, contract, preferred_element_type=jnp.float32), "grp", 0
    )
    grad_first = summed_on_arrival(first_share, "dev", 0)
    columns = active
    second_share = summed_on_arrival(
        lax.dot_general(columns, out_grad, contract, preferred_element_type=jnp.float32), "grp", 0
    )
    grad_second = summed_on_arrival(second_share, "dev", 0)
    owned = emb_table.shape[0]
    local_grad = segment_rows(got_grads, got_ids, owned)
    table_grad = lax.psum(local_grad, "grp")
    new_state = adagrad_state + table_grad * table_grad
    new_table = emb_table - learn_rate * table_grad / (jnp.sqrt(new_state) + epsilon)
    return (grad_first, grad_second, new_table, new_state)


def solution(mesh):
    in_specs = (
        P(("grp", "dev"), None),
        P(("grp", "dev"), None),
        P(("grp", "dev"), None),
        P(),
        P(("grp", "dev"), None),
        P(("grp", "dev")),
        P(("grp", "dev")),
        P("dev", None),
        P("dev", None),
    )
    out_specs = (P(("grp", "dev"), None), P(("grp", "dev"), None), P("dev", None), P("dev", None))
    return jax.shard_map(
        on_device, mesh=mesh, in_specs=in_specs, out_specs=out_specs, check_vma=False
    )
```

profile of v0, /device:TPU:0, one launch (start us, length us, event | category | flops | bytes accessed | tf_op | source)
XLA Modules:
  0.0 185.0 jit_solution(922383778627406462)
XLA Ops:
  7.2 0.0 copy-start
  7.2 0.9 iota_compare_fusion
  8.1 0.1 lt.23
  8.1 0.7 broadcast_select_fusion
  8.8 0.1 all_to_all.32
  8.9 16.8 %all_to_all.44 = s32[32,64,1]{1,2,0:T(1,128)S(1)} all-to-all(s32[32,64,1]{1,2,0:T(1,128)S(1)} %bitcast.33), channel_id=1, replica_groups=mesh['grp'=4,'dev'=32] {'dev'}, dimensions={0} | all-to-all | bytes 16384 | tf_op jit(solution)/shard_map/all_to_all | solution.py:54
  25.8 3.9 %all-to-all-start.5 = ((bf16[32,64,128]{2,1,0:T(8,128)(2,1)}), bf16[32,64,128]{2,1,0:T(8,128)(2,1)S(1)}, u32[]{:S(2)}, u32[]{:S(2)}) async-start(bf16[32,64,128]{2,1,0:T(8,128)(2,1)} %bitcast.31), calls=%async_computation.5 | async-start | bytes 1048576 | tf_op jit(solution)/shard_map/all_to_all | solution.py:53
  29.7 0.0 copy-done
  29.7 5.9 %fusion.11 = f32[1024,512]{1,0:T(8,128)} fusion(bf16[2048,512]{1,0:T(8,128)(2,1)S(1)} %copy-done, bf16[2048,1024]{1,0:T(8,128)(2,1)} %param.12), kind=kOutput, calls=%fused_computation.9 | convolution fusion | flops 2149580800 | bytes 8388608 | tf_op jit(solution)/shard_map/dot_general | solution.py:63
  35.6 5.2 %all-to-all-done.5 = bf16[32,64,128]{2,1,0:T(8,128)(2,1)S(1)} async-done(((bf16[32,64,128]{2,1,0:T(8,128)(2,1)}), bf16[32,64,128]{2,1,0:T(8,128)(2,1)S(1)}, u32[]{:S(2)}, u32[]{:S(2)}) %all-to-all-start.5) | async-done | bytes 524320 | tf_op jit(solution)/shard_map/all_to_all | solution.py:53
  40.7 4.9 %all-to-all-start.2 = ((f32[4,256,512]{2,1,0:T(8,128)}), f32[4,256,512]{2,1,0:T(8,128)}, u32[]{:S(2)}, u32[]{:S(2)}) async-start(f32[4,256,512]{2,1,0:T(8,128)} %bitcast.29), calls=%async_computation.2 | async-start | bytes 4194304 | tf_op jit(solution)/shard_map/all_to_all | solution.py:17
  45.6 13.2 %fusion.10 = f32[1024,1024]{0,1:T(8,128)} fusion(bf16[2048,1024]{1,0:T(8,128)(2,1)} %param.11, bf16[2048,1024]{1,0:T(8,128)(2,1)} %param.12, bf16[2048,512]{1,0:T(8,128)(2,1)S(1)} %copy-done, bf16[1024,512]{1,0:T(8,128)(2,1)} %param.14), kind=kOutput, calls=%fused_computation.8 | convolution fusion | flops 6448742400 | bytes 15728640 | tf_op jit(solution)/shard_map/dot_general | solution.py:58
  58.8 14.1 %all-to-all-done.2 = f32[4,256,512]{2,1,0:T(8,128)} async-done(((f32[4,256,512]{2,1,0:T(8,128)}), f32[4,256,512]{2,1,0:T(8,128)}, u32[]{:S(2)}, u32[]{:S(2)}) %all-to-all-start.2) | async-done | bytes 2097184 | tf_op jit(solution)/shard_map/all_to_all | solution.py:17
  72.9 4.9 %all-to-all-start = ((f32[4,256,1024]{2,1,0:T(8,128)}), f32[4,256,1024]{2,1,0:T(8,128)}, u32[]{:S(2)}, u32[]{:S(2)}) async-start(f32[4,256,1024]{2,1,0:T(8,128)} %bitcast.27), calls=%async_computation | async-start | bytes 8388608 | tf_op jit(solution)/shard_map/all_to_all | solution.py:17
  77.7 0.0 all-reduce.2.cloned.1.call-start
  77.8 0.5 broadcast.31
  78.3 0.7 reduce.3
  79.0 0.1 all_to_all.34
  79.1 10.9 %while.10 = (s32[]{:T(128)}, f32[4,512,128]{2,1,0:T(8,128)}, s32[4]{0:T(128)S(1)}, s32[2048]{0:T(1024)S(1)}, bf16[2048,128]{1,0:T(8,128)(2,1)S(1)}, /*index=5*/s32[]{:T(128)}, s32[1]{0:T(128)}) while((s32[]{:T(128)}, f32[4,512,128]{2,1,0:T(8,128)}, s32[4]{0:T(128)S(1)}, s32[2048]{0:T(1024)S(1)}, bf16[2048,128]{1,0:T(8,128)(2,1)S(1)}, ...), condition=%wide.region_5.6_spmd, body=%wide.region_4.5_spmd.sunk | while | flops 269484544 | bytes 798837 | solution.py:29
  79.1 0.6 dynamic_slice.5
  80.3 1.5 fusion.31
  81.8 0.6 dynamic_slice.5
  83.0 1.5 fusion.31
  84.5 0.6 dynamic_slice.5
  85.7 1.5 fusion.31
  87.2 0.6 dynamic_slice.5
  88.5 1.5 fusion.31
  89.9 0.0 all-reduce.2.cloned.1.call-update
  89.9 2.7 %reduce_sum.38 = f32[256,512]{1,0:T(8,128)} reduce(f32[4,256,512]{2,1,0:T(8,128)} %all-to-all-done.2, f32[]{:T(128)} %constant.5.clone.1), dimensions={0}, to_apply=%region_2.3 | reduce | flops 393216 | bytes 2621444 | tf_op jit(solution)/shard_map/reduce_sum | solution.py:18
  92.6 49.4 %all-to-all-done = f32[4,256,1024]{2,1,0:T(8,128)} async-done(((f32[4,256,1024]{2,1,0:T(8,128)}), f32[4,256,1024]{2,1,0:T(8,128)}, u32[]{:S(2)}, u32[]{:S(2)}) %all-to-all-start) | async-done | bytes 4194336 | tf_op jit(solution)/shard_map/all_to_all | solution.py:17
  142.0 3.9 %all-to-all-start.3 = ((f32[32,8,512]{2,1,0:T(8,128)}), f32[32,8,512]{2,1,0:T(8,128)S(1)}, u32[]{:S(2)}, u32[]{:S(2)}) async-start(f32[32,8,512]{2,1,0:T(8,128)} %bitcast.6), calls=%async_computation.3 | async-start | bytes 1048576 | tf_op jit(solution)/shard_map/all_to_all | solution.py:17
  145.9 3.7 %reduce_sum.36 = f32[256,1024]{1,0:T(8,128)} reduce(f32[4,256,1024]{2,1,0:T(8,128)} %all-to-all-done, f32[]{:T(128)} %constant.5.clone.1), dimensions={0}, to_apply=%region_0.1 | reduce | flops 786432 | bytes 5242884 | tf_op jit(solution)/shard_map/reduce_sum | solution.py:18
  149.6 7.4 %all-to-all-done.3 = f32[32,8,512]{2,1,0:T(8,128)S(1)} async-done(((f32[32,8,512]{2,1,0:T(8,128)}), f32[32,8,512]{2,1,0:T(8,128)S(1)}, u32[]{:S(2)}, u32[]{:S(2)}) %all-to-all-start.3) | async-done | bytes 524320 | tf_op jit(solution)/shard_map/all_to_all | solution.py:17
  156.9 0.0 copy-start.1
  156.9 0.8 copy-done.1
  157.7 3.9 %all-to-all-start.1 = ((f32[32,8,1024]{2,1,0:T(8,128)}), f32[32,8,1024]{2,1,0:T(8,128)S(1)}, u32[]{:S(2)}, u32[]{:S(2)}) async-start(f32[32,8,1024]{2,1,0:T(8,128)} %bitcast.28), calls=%async_computation.1 | async-start | bytes 2097152 | tf_op jit(solution)/shard_map/all_to_all | solution.py:17
  161.6 0.0 all-reduce.2.cloned.1.call-done
  161.7 3.6 %divide_subtract_fusion = (f32[2048,128]{1,0:T(8,128)}, f32[2048,128]{1,0:T(8,128)}) fusion(f32[2048,128]{1,0:T(8,128)} %param.18, f32[2048,128]{1,0:T(8,128)} %all-reduce.2.cloned.1.call-done, f32[2048,128]{1,0:T(8,128)} %param.19), kind=kLoop, calls=%fused_computation.15 | loop fusion | flops 1572864 | bytes 5242880 | tf_op jit(solution)/shard_map/sub | solution.py:70
  165.3 1.7 reduce_sum.39
  167.0 10.5 %all-to-all-done.1 = f32[32,8,1024]{2,1,0:T(8,128)S(1)} async-done(((f32[32,8,1024]{2,1,0:T(8,128)}), f32[32,8,1024]{2,1,0:T(8,128)S(1)}, u32[]{:S(2)}, u32[]{:S(2)}) %all-to-all-start.1) | async-done | bytes 1048608 | tf_op jit(solution)/shard_map/all_to_all | solution.py:17
  177.5 0.7 reduce_sum.37
  (6 shorter events, 0.0 us)
Async XLA Ops:
  7.2 22.5 %copy-start = (bf16[2048,512]{1,0:T(8,128)(2,1)S(1)}, bf16[2048,512]{1,0:T(8,128)(2,1)}, u32[]{:S(2)}) copy-start(bf16[2048,512]{1,0:T(8,128)(2,1)} %param.13) | copy-start | bytes 6291460
  25.8 15.0 %all-to-all-start.5 = ((bf16[32,64,128]{2,1,0:T(8,128)(2,1)}), bf16[32,64,128]{2,1,0:T(8,128)(2,1)S(1)}, u32[]{:S(2)}, u32[]{:S(2)}) async-start(bf16[32,64,128]{2,1,0:T(8,128)(2,1)} %bitcast.31), calls=%async_computation.5 | async-start | bytes 1048576 | tf_op jit(solution)/shard_map/all_to_all | solution.py:53
  40.7 32.1 %all-to-all-start.2 = ((f32[4,256,512]{2,1,0:T(8,128)}), f32[4,256,512]{2,1,0:T(8,128)}, u32[]{:S(2)}, u32[]{:S(2)}) async-start(f32[4,256,512]{2,1,0:T(8,128)} %bitcast.29), calls=%async_computation.2 | async-start | bytes 4194304 | tf_op jit(solution)/shard_map/all_to_all | solution.py:17
  72.9 69.1 %all-to-all-start = ((f32[4,256,1024]{2,1,0:T(8,128)}), f32[4,256,1024]{2,1,0:T(8,128)}, u32[]{:S(2)}, u32[]{:S(2)}) async-start(f32[4,256,1024]{2,1,0:T(8,128)} %bitcast.27), calls=%async_computation | async-start | bytes 8388608 | tf_op jit(solution)/shard_map/all_to_all | solution.py:17
  77.7 83.9 %all-reduce.2.cloned.1.call-start = ((), (), s32[]{:S(2)}) async-start(), calls=%async_computation.6 | async-start | bytes 2097152 | tf_op jit(solution)/shard_map/psum | solution.py:68
  142.0 15.0 %all-to-all-start.3 = ((f32[32,8,512]{2,1,0:T(8,128)}), f32[32,8,512]{2,1,0:T(8,128)S(1)}, u32[]{:S(2)}, u32[]{:S(2)}) async-start(f32[32,8,512]{2,1,0:T(8,128)} %bitcast.6), calls=%async_computation.3 | async-start | bytes 1048576 | tf_op jit(solution)/shard_map/all_to_all | solution.py:17
  156.9 0.8 copy-start.1
  157.7 19.8 %all-to-all-start.1 = ((f32[32,8,1024]{2,1,0:T(8,128)}), f32[32,8,1024]{2,1,0:T(8,128)S(1)}, u32[]{:S(2)}, u32[]{:S(2)}) async-start(f32[32,8,1024]{2,1,0:T(8,128)} %bitcast.28), calls=%async_computation.1 | async-start | bytes 2097152 | tf_op jit(solution)/shard_map/all_to_all | solution.py:17
Sparse Core Ops, SparseCore 0:
  90.1 54.2 all-reduce.1
where the time goes:
time: 186 us; the launch traced here: 185 us
  waiting for transfers between devices  86.4 us (46%)
  matrix products  25 us (13%)
  starting transfers between devices  21.5 us (12%)
  blocking collectives  16.8 us (9%)
  other arithmetic  14.6 us (8%)
  between operations  14.1 us (8%)
  local copies, waits for them, and re-layouts  3.88 us (2%)
  loops' own time  2.64 us (1%)
    all_to_all x4, waiting for transfers between devices, summed_on_arrival(): lax.all_to_all(split_up(array, dim, devices), axis, 0, 0, tiled=True)  81.2 us
    all_to_all x4, starting transfers between devices, summed_on_arrival(): lax.all_to_all(split_up(array, dim, devices), axis, 0, 0, tiled=True)  17.5 us
    all_to_all x1, blocking collectives, on_device(): lax.all_to_all(sent_ids, 'dev', split_axis=0, concat_axis=0, tiled=True)  16.8 us
    dot_general x1, matrix products, on_device(): lax.dot_general(columns, d_hidden, contract, preferred_element_type=jnp.f...  13.2 us
    reduce_sum x4, other arithmetic, summed_on_arrival(): return jnp.sum(blocks, axis=0)  8.73 us
    dot_general x1, matrix products, on_device(): lax.dot_general(columns, out_grad, contract, preferred_element_type=jnp.f...  5.9 us
    dot_general x4, matrix products, one_block(): return jnp.dot(onehot, gathered, preferred_element_type=jnp.float32)  5.87 us
    all_to_all x1, waiting for transfers between devices, on_device(): lax.all_to_all(row_grads, 'dev', split_axis=0, concat_axis=0, tiled=True)  5.16 us
  transfers between devices with their start and end apart: 6, of which 5 were waited for; matrix products, arithmetic and copies ran while one was open for 22% of the time, Pallas kernels for 0%

commit v1 on v0

v1 whole, which is shorter than its diff:
```python
import jax
import jax.numpy as jnp
from jax import lax
from jax.experimental import pallas as pl
from jax.experimental.pallas import tpu as pltpu
from jax.sharding import Mesh, PartitionSpec as P

learn_rate = 0.5
epsilon = 1e-08
LOW = 64
CHIPS = ("zh", "y", "x", "zl")
DEV = ("y", "x", "zl")
SWAP = ((0, 1), (1, 0))
WIDTH = 256
ROWS_CONTRACTED = (((0,), (0,)), ((), ()))
LANES_CONTRACTED = (((1,), (1,)), ((), ()))
IN_SMEM = pl.BlockSpec(memory_space=pltpu.SMEM)
IN_VMEM = pl.BlockSpec(memory_space=pltpu.VMEM)
IN_HBM = pl.BlockSpec(memory_space=pltpu.HBM)


def in_vmem(array):
    return pltpu.with_memory_space_constraint(array, pltpu.VMEM)


def in_hbm(array):
    return pltpu.with_memory_space_constraint(array, pltpu.HBM)


def pack_kernel(counts_from, ids_from, grads, out, counts, ids, sems):
    blocks, height = out.shape[:2]
    capacity = height - 8
    counts_copy = pltpu.make_async_copy(counts_from, counts, sems.at[0])
    ids_copy = pltpu.make_async_copy(ids_from, ids, sems.at[1])
    grads_copy = pltpu.make_async_copy(grads, out.at[:, pl.ds(0, capacity), :], sems.at[2])
    counts_copy.start()
    ids_copy.start()
    grads_copy.start()
    lane = lax.broadcasted_iota(jnp.int32, (1, 128), 1)
    row = lax.broadcasted_iota(jnp.int32, (8, 128), 0)
    counts_copy.wait()
    ids_copy.wait()
    for block in range(blocks):
        here = ids[pl.ds(block // 2, 1), :]
        turned = pltpu.roll(here, capacity, 1)
        twice = jnp.where((lane < capacity) == (block % 2 == 0), here, turned)
        usable = lax.rem(lane, capacity) < counts[block]
        high = jnp.where(usable, lax.shift_right_logical(twice, 6), 2 * LOW)
        low = jnp.where(usable, lax.bitwise_and(twice, LOW - 1), 0)
        tail = jnp.where(row == 0, high, jnp.where(row == 1, low, 0))
        out[block, pl.ds(capacity, 8), :] = tail.astype(jnp.float32).astype(out.dtype)
    grads_copy.wait()


def packed(counts, ids, grads):
    blocks, width = counts.shape[0], grads.shape[1]
    capacity = grads.shape[0] // blocks
    ids = ids.reshape(-1, 128)
    return pl.pallas_call(
        pack_kernel,
        out_shape=pltpu.VMEM((blocks, capacity + 8, width), grads.dtype),
        in_specs=[IN_HBM] * 3,
        out_specs=IN_VMEM,
        scratch_shapes=[
            pltpu.SMEM((blocks,), jnp.int32),
            pltpu.VMEM(ids.shape, jnp.int32),
            pltpu.SemaphoreType.DMA((3,)),
        ],
        compiler_params=pltpu.CompilerParams(vmem_limit_bytes=8 << 20),
        cost_estimate=pl.CostEstimate(flops=1000000, transcendentals=0, bytes_accessed=1 << 20),
        name="pack_rows",
    )(in_hbm(counts), in_hbm(ids), in_hbm(grads.reshape(blocks, capacity, width)))


def scatter_kernel(core_ref, own, other, out, acc):
    rows = acc.shape[0]
    wanted = core_ref[0] * rows + lax.broadcasted_iota(jnp.int32, (rows, 128), 0)
    lane = lax.broadcasted_iota(jnp.int32, (1, 128), 1)

    def ids_of(blocks, block):
        tail = blocks[block, pl.ds(64, 8), :].astype(jnp.float32)
        return (tail[0:1] * LOW + tail[1:2]).astype(jnp.int32)

    first = True
    for blocks in (own, other):
        for step in range(blocks.shape[0] // 4):
            hot = []
            for block in (4 * step, 4 * step + 2):
                ids = jnp.where(lane < 64, ids_of(blocks, block), ids_of(blocks, block + 1))
                same = wanted == jnp.broadcast_to(ids, (rows, 128))
                hot.append(same.astype(jnp.float32).astype(jnp.bfloat16))
            values = blocks[pl.ds(4 * step, 4), pl.ds(0, 64), :].reshape(256, 128)
            part = jnp.dot(
                jnp.concatenate(hot, axis=1), values, preferred_element_type=jnp.float32
            )
            if first:
                acc[...] = part
                first = False
            else:
                acc[...] += part
    out[...] = acc[...].astype(out.dtype)


def scattered(core, own, other, rows):
    return pl.pallas_call(
        scatter_kernel,
        out_shape=jax.ShapeDtypeStruct((rows, own.shape[2]), jnp.bfloat16),
        in_specs=[IN_SMEM, IN_VMEM, IN_VMEM],
        out_specs=IN_VMEM,
        scratch_shapes=[pltpu.VMEM((rows, own.shape[2]), jnp.float32)],
        compiler_params=pltpu.CompilerParams(vmem_limit_bytes=16 << 20),
        cost_estimate=pl.CostEstimate(flops=1000000000, transcendentals=0, bytes_accessed=1 << 20),
        name="scatter_rows",
    )(core, own, other)


def update_kernel(core_ref, near, far, near_other, far_other, table, state, new_table, new_state):
    half = near.shape[0]

    def apply(place, first, second):
        rows = pl.ds(pl.multiple_of(place * half, half), half)
        grad = first[...].astype(jnp.float32) + second[...].astype(jnp.float32)
        summed = state[rows, :] + grad * grad
        new_state[rows, :] = summed
        new_table[rows, :] = table[rows, :] - learn_rate * grad / (jnp.sqrt(summed) + epsilon)

    apply(core_ref[0], near, far)
    apply(1 - core_ref[0], near_other, far_other)


def updated(core, near, far, near_other, far_other, table, state):
    return pl.pallas_call(
        update_kernel,
        out_shape=(
            jax.ShapeDtypeStruct(table.shape, table.dtype),
            jax.ShapeDtypeStruct(state.shape, state.dtype),
        ),
        in_specs=[IN_SMEM] + [IN_VMEM] * 6,
        out_specs=(IN_VMEM, IN_VMEM),
        compiler_params=pltpu.CompilerParams(vmem_limit_bytes=16 << 20),
        cost_estimate=pl.CostEstimate(flops=2000000, transcendentals=0, bytes_accessed=5 << 20),
        name="update_rows",
    )(core, near, far, near_other, far_other, table, state)


def columns_at(tile, core):
    return pl.ds(pl.multiple_of((2 * tile + core) * WIDTH, WIDTH), WIDTH)


def column_tiles(source, kept, sems, core):
    wanted = [(0, 1 - core), (1, 1 - core), (0, core), (1, core)]
    return [
        pltpu.make_async_copy(
            source.at[:, columns_at(tile, of)],
            kept.at[place],
            sems.at[place],
        )
        for place, (tile, of) in enumerate(wanted)
    ]


def transposed_dot(left, right):
    return lax.dot_general(left, right, ROWS_CONTRACTED, preferred_element_type=jnp.float32)


def active_of(pre):
    return jnp.maximum(pre, jnp.zeros((), pre.dtype))


def theirs_kernel(
    core_ref, grad, weight, hidden, given, d_out, theirs, grad_kept, given_kept, hidden_kept,
    weight_kept, weight_sem, grad_sems, hidden_sems, given_sems,
):
    steps = grad_sems.shape[0]
    height = grad.shape[0] // steps
    core = core_ref[0]
    wide = d_out.shape[1]
    weight_copy = pltpu.make_async_copy(weight, weight_kept, weight_sem)

    def part(source, kept, sems, i):
        rows = pl.ds(i * height, height)
        return pltpu.make_async_copy(source.at[rows, :], kept.at[rows, :], sems.at[i])

    given_copies = column_tiles(given, given_kept, given_sems, core)

    def start_part(i):
        part(grad, grad_kept, grad_sems, i).start()
        part(hidden, hidden_kept, hidden_sems, i).start()

    weight_copy.start()
    start_part(0)
    start_part(1)
    weight_copy.wait()
    for i in range(steps):
        rows = pl.ds(i * height, height)
        part(grad, grad_kept, grad_sems, i).wait()
        part(hidden, hidden_kept, hidden_sems, i).wait()
        if i + 2 < steps:
            start_part(i + 2)
        if steps <= i + 4:
            given_copies[i + 4 - steps].start()
        back = lax.dot_general(
            grad_kept[rows, :], weight_kept[...], LANES_CONTRACTED,
            preferred_element_type=jnp.float32,
        )
        d_out[rows, :] = jnp.where(hidden_kept[rows, :] > 0, back, 0.0).astype(d_out.dtype)

    for place in range(2):
        rows = pl.ds(place * WIDTH, WIDTH)
        given_copies[place].wait()
        theirs[rows, pl.ds(0, wide)] = transposed_dot(given_kept[place], d_out[...]).astype(
            theirs.dtype
        )
    for place in range(2):
        rows = pl.ds(place * WIDTH, WIDTH)
        theirs[rows, pl.ds(wide, grad.shape[1])] = transposed_dot(
            active_of(hidden_kept[:, columns_at(place, 1 - core)]), grad_kept[...]
        ).astype(theirs.dtype)
    for copy in given_copies[2:]:
        copy.wait()


def mine_kernel(core_ref, given_kept, d_hidden, hidden_kept, grad, mine):
    core = core_ref[0]
    wide = d_hidden.shape[1]
    for place in range(2):
        rows = pl.ds(place * WIDTH, WIDTH)
        mine[rows, pl.ds(0, wide)] = transposed_dot(given_kept[2 + place], d_hidden[...])
        mine[rows, pl.ds(wide, grad.shape[1])] = transposed_dot(
            active_of(hidden_kept[:, columns_at(place, core)]), grad[...]
        )


def theirs_of(core, grad, weight, hidden, given):
    tokens, steps = grad.shape[0], 4
    columns = hidden.shape[1] + grad.shape[1]
    return pl.pallas_call(
        theirs_kernel,
        out_shape=(
            pltpu.VMEM(hidden.shape, jnp.bfloat16),
            pltpu.VMEM((2 * WIDTH, columns), jnp.bfloat16),
            pltpu.VMEM(grad.shape, grad.dtype),
            pltpu.VMEM((4, tokens, WIDTH), given.dtype),
            pltpu.VMEM(hidden.shape, hidden.dtype),
        ),
        in_specs=[IN_SMEM] + [IN_HBM] * 4,
        out_specs=(IN_VMEM,) * 5,
        scratch_shapes=[
            pltpu.VMEM(weight.shape, weight.dtype),
            pltpu.SemaphoreType.DMA,
            pltpu.SemaphoreType.DMA((steps,)),
            pltpu.SemaphoreType.DMA((steps,)),
            pltpu.SemaphoreType.DMA((4,)),
        ],
        compiler_params=pltpu.CompilerParams(vmem_limit_bytes=24 << 20),
        cost_estimate=pl.CostEstimate(flops=5400000000, transcendentals=0, bytes_accessed=11 << 20),
        name="theirs_of",
    )(core, in_hbm(grad), in_hbm(weight), in_hbm(hidden), in_hbm(given))


def mine_of(core, given, d_hidden, hidden, grad):
    columns = d_hidden.shape[1] + grad.shape[1]
    return pl.pallas_call(
        mine_kernel,
        out_shape=pltpu.VMEM((2 * WIDTH, columns), jnp.float32),
        in_specs=[IN_SMEM] + [IN_VMEM] * 4,
        out_specs=IN_VMEM,
        compiler_params=pltpu.CompilerParams(vmem_limit_bytes=24 << 20),
        cost_estimate=pl.CostEstimate(flops=3200000000, transcendentals=0, bytes_accessed=2 << 20),
        name="mine_of",
    )(core, in_vmem(given), in_vmem(d_hidden), in_vmem(hidden), in_vmem(grad))


def join_kernel(mine, arrived, out):
    out[...] = (mine[...] + arrived[...].astype(jnp.float32)).astype(out.dtype)


def joined(mine, arrived):
    return pl.pallas_call(
        join_kernel,
        out_shape=pltpu.VMEM(mine.shape, jnp.bfloat16),
        in_specs=[IN_VMEM, IN_VMEM],
        out_specs=IN_VMEM,
        compiler_params=pltpu.CompilerParams(vmem_limit_bytes=16 << 20),
        cost_estimate=pl.CostEstimate(flops=1000000, transcendentals=0, bytes_accessed=2 << 20),
        name="join_halves",
    )(in_vmem(mine), in_vmem(arrived))


def total_kernel(blocks, first, second):
    wide = first.shape[1]
    total = blocks[0].astype(jnp.float32)
    for chip in range(1, blocks.shape[0]):
        total += blocks[chip].astype(jnp.float32)
    first[...] = total[:, :wide]
    second[...] = total[:, wide:]


def totals(blocks, wide):
    rows, columns = blocks.shape[1:]
    return pl.pallas_call(
        total_kernel,
        out_shape=(
            jax.ShapeDtypeStruct((rows, wide), jnp.float32),
            jax.ShapeDtypeStruct((rows, columns - wide), jnp.float32),
        ),
        in_specs=[IN_VMEM],
        out_specs=(IN_VMEM, IN_VMEM),
        compiler_params=pltpu.CompilerParams(vmem_limit_bytes=16 << 20),
        cost_estimate=pl.CostEstimate(flops=1000000, transcendentals=0, bytes_accessed=2 << 20),
        name="total_blocks",
    )(in_vmem(blocks))


def to_owners(share):
    chips = lax.axis_size(CHIPS)
    blocks = share.reshape(chips, share.shape[0] // chips, share.shape[1])
    return lax.all_to_all(blocks, CHIPS, 0, 0, tiled=True)


def on_device(
    layer_input,
    hidden_pre,
    out_grad,
    second_weight,
    row_grads,
    row_ids,
    block_counts,
    emb_table,
    adagrad_state,
):
    at_core = lax.axis_index("c").astype(jnp.int32).reshape(1)
    own = lax.all_to_all(packed(block_counts, row_ids, row_grads), DEV, 0, 0, tiled=True)

    d_hidden, theirs, grad_kept, given_kept, hidden_kept = theirs_of(
        at_core, out_grad, second_weight, hidden_pre, layer_input
    )
    arrived = lax.ppermute(theirs, "c", SWAP)
    mine = mine_of(at_core, given_kept, d_hidden, hidden_kept, grad_kept)
    share = joined(mine, arrived)
    blocks = to_owners(share)
    grad_first, grad_second = totals(blocks, hidden_pre.shape[1])

    other = lax.ppermute(own, "c", SWAP)
    near = scattered(at_core, own, other, emb_table.shape[0] // 2)
    far = lax.ppermute(near, "zh", SWAP)
    near_other = lax.ppermute(near, "c", SWAP)
    far_other = lax.ppermute(far, "c", SWAP)
    new_table, new_state = updated(
        at_core, near, far, near_other, far_other, emb_table, adagrad_state
    )
    return (grad_first, grad_second, new_table, new_state)


def solution(mesh):
    names = ("zh", "c", "y", "x", "zl")
    split = Mesh(mesh.devices.reshape(2, 2, 4, 4, 2), names)
    every = P(names, None)
    in_specs = (
        every,
        every,
        every,
        P(),
        every,
        P(names),
        P(names),
        P(DEV, None),
        P(DEV, None),
    )
    out_specs = (every, every, P(DEV, None), P(DEV, None))
    return jax.shard_map(
        on_device, mesh=split, in_specs=in_specs, out_specs=out_specs, check_vma=False
    )
```

time: 186 us -> 86 us (0.46)
  waiting for transfers between devices: 86.4 us -> 25.4 us
  matrix products: 25 us -> 0 us
  Pallas kernels: 0 us -> 23.1 us
  blocking collectives: 16.8 us -> 0 us
  other arithmetic: 14.6 us -> 0 us
  between operations: 14.1 us -> 0.73 us
  local copies, waits for them, and re-layouts: 3.88 us -> 12.5 us
  loops' own time: 2.64 us -> 0 us
    all_to_all x5 -> x2, waiting for transfers between devices: 86.4 us -> 0.54 us  [the longest x1 0.54 us: on_device(): lax.all_to_all(packed(block_counts, row_ids, row_grads), DEV, 0, 0, tiled...]
    dot_general x6 -> x0, matrix products: 25 us -> none  [the longest x1 13.2 us: on_device(): lax.dot_general(columns, d_hidden, contract, preferred_element_type=jnp.f...]
    ppermute x0 -> x5, waiting for transfers between devices: none -> 24.8 us  [the longest x1 21.3 us: on_device(): far = lax.ppermute(near, 'zh', SWAP)]
    pallas_call x0 -> x7, Pallas kernels: none -> 23.1 us  [the longest x1 9.82 us: theirs_of(): pl.pallas_call(theirs_kernel, out_shape=(pltpu.VMEM(hidden.shape, jnp.bfl...]
    all_to_all x1 -> x0, blocking collectives: 16.8 us -> none  [on_device(): lax.all_to_all(sent_ids, 'dev', split_axis=0, concat_axis=0, tiled=True)]
    unnamed x4 -> x16, local copies, waits for them, and re-layouts: 0.8 us -> 12.5 us
    reduce_sum x4 -> x0, other arithmetic: 8.73 us -> none  [summed_on_arrival(): return jnp.sum(blocks, axis=0)]
    sub x1 -> x0, other arithmetic: 3.64 us -> none  [on_device(): emb_table - learn_rate * table_grad / (jnp.sqrt(new_state) + epsilon)]
  transfers between devices with their start and end apart: 6 -> 7, of which waited for: 5 -> 4; matrix products, arithmetic and copies ran while one was open for 22% -> 0% of each run, Pallas kernels for 0% -> 15%
where the time goes in v1:
time: 86 us; the launch traced here: 84.5 us
  waiting for transfers between devices  25.4 us (30%)
  Pallas kernels  23.1 us (27%)
  starting transfers between devices  22.8 us (27%)
  local copies, waits for them, and re-layouts  12.5 us (15%)
    ppermute x1, waiting for transfers between devices, on_device(): far = lax.ppermute(near, 'zh', SWAP)  21.3 us
    unnamed x16, local copies, waits for them, and re-layouts  12.5 us
    all_to_all x1, starting transfers between devices, to_owners(): return lax.all_to_all(blocks, CHIPS, 0, 0, tiled=True)  10.6 us
    pallas_call x1, Pallas kernels, theirs_of(): pl.pallas_call(theirs_kernel, out_shape=(pltpu.VMEM(hidden.shape, jnp.bfl...  9.82 us
    all_to_all x1, starting transfers between devices, on_device(): lax.all_to_all(packed(block_counts, row_ids, row_grads), DEV, 0, 0, tiled...  8.79 us
    pallas_call x1, Pallas kernels, mine_of(): pl.pallas_call(mine_kernel, out_shape=pltpu.VMEM((2 * WIDTH, columns), jn...  3.48 us
    ppermute x1, starting transfers between devices, on_device(): far = lax.ppermute(near, 'zh', SWAP)  3.25 us
    pallas_call x1, Pallas kernels, joined(): pl.pallas_call(join_kernel, out_shape=pltpu.VMEM(mine.shape, jnp.bfloat16...  2.99 us
  transfers between devices with their start and end apart: 7, of which 4 were waited for; matrix products, arithmetic and copies ran while one was open for 0% of the time, Pallas kernels for 15%

profile of v1, /device:TPU:0, one launch (start us, length us, event | category | flops | bytes accessed | tf_op | source)
XLA Modules:
  0.0 84.5 jit_solution(6049687459279421276)
XLA Ops:
  0.6 9.8 %theirs_of.1 = (bf16[2048,1024]{1,0:T(8,128)(2,1)S(1)}, bf16[512,1536]{1,0:T(8,128)(2,1)}, bf16[2048,512]{1,0:T(8,128)(2,1)S(1)}, bf16[4,2048,256]{2,1,0:T(8,128)(2,1)S(1)}, bf16[2048,1024]{1,0:T(8,128)(2,1)S(1)}) custom-call(s32[1]{0:T(128)} %bitcast.core_ref, bf16[2048,512]{1,0:T(8,128)(2,1)} %grad.1, bf16[1024,512]{1,0:T(8,128)(2,1)} %weight.1, ...), custom_call_target="tpu_custom_call" | custom-call | flops 5400000000 | bytes 11534336 | tf_op jit(solution)/shard_map/theirs_of/pallas_call | solution.py:237
  10.5 0.0 copy-start
  10.5 2.0 %copy-done = bf16[2048,1024]{1,0:T(8,128)(2,1)} copy-done((bf16[2048,1024]{1,0:T(8,128)(2,1)}, bf16[2048,1024]{1,0:T(8,128)(2,1)S(1)}, u32[]{:S(2)}) %copy-start) | copy-done | bytes 4194328
  12.5 0.0 copy-start.2
  12.5 2.0 %copy-done.2 = bf16[4,2048,256]{2,1,0:T(8,128)(2,1)} copy-done((bf16[4,2048,256]{2,1,0:T(8,128)(2,1)}, bf16[4,2048,256]{2,1,0:T(8,128)(2,1)S(1)}, u32[]{:S(2)}) %copy-start.2) | copy-done | bytes 4194328
  14.4 0.0 copy-start.4
  14.4 2.0 %copy-done.4 = bf16[2048,1024]{1,0:T(8,128)(2,1)} copy-done((bf16[2048,1024]{1,0:T(8,128)(2,1)}, bf16[2048,1024]{1,0:T(8,128)(2,1)S(1)}, u32[]{:S(2)}) %copy-start.4) | copy-done | bytes 4194328
  16.4 0.0 collective-permute-start
  16.4 1.9 %pack_rows.1 = bf16[32,72,128]{2,1,0:T(8,128)(2,1)} custom-call(s32[32]{0:T(128)} %counts_from.1, s32[16,128]{1,0:T(8,128)} %bitcast.5, bf16[32,64,128]{2,1,0:T(8,128)(2,1)} %bitcast.4), custom_call_target="tpu_custom_call" | custom-call | flops 1000000 | bytes 1048576 | tf_op jit(solution)/shard_map/pack_rows/pallas_call | solution.py:59
  18.3 8.8 %all-to-all-start.1 = ((bf16[32,72,128]{2,1,0:T(8,128)(2,1)}), bf16[32,72,128]{2,1,0:T(8,128)(2,1)S(1)}, u32[]{:S(2)}, u32[]{:S(2)}) async-start(bf16[32,72,128]{2,1,0:T(8,128)(2,1)} %pack_rows.1), calls=%async_computation.1 | async-start | bytes 1179648 | tf_op jit(solution)/shard_map/all_to_all | solution.py:333
  27.1 0.0 copy-start.1
  27.1 2.2 %copy-done.1 = bf16[2048,1024]{1,0:T(8,128)(2,1)S(1)} copy-done((bf16[2048,1024]{1,0:T(8,128)(2,1)S(1)}, bf16[2048,1024]{1,0:T(8,128)(2,1)}, u32[]{:S(2)}) %copy-start.1) | copy-done | bytes 4194328
  29.3 0.0 copy-start.3
  29.3 2.2 %copy-done.3 = bf16[4,2048,256]{2,1,0:T(8,128)(2,1)S(1)} copy-done((bf16[4,2048,256]{2,1,0:T(8,128)(2,1)S(1)}, bf16[4,2048,256]{2,1,0:T(8,128)(2,1)}, u32[]{:S(2)}) %copy-start.3) | copy-done | bytes 4194328
  31.5 0.0 copy-start.5
  31.5 2.2 %copy-done.5 = bf16[2048,1024]{1,0:T(8,128)(2,1)S(1)} copy-done((bf16[2048,1024]{1,0:T(8,128)(2,1)S(1)}, bf16[2048,1024]{1,0:T(8,128)(2,1)}, u32[]{:S(2)}) %copy-start.5) | copy-done | bytes 4194328
  33.7 3.5 %mine_of.1.mine = f32[512,1536]{1,0:T(8,128)S(1)} custom-call(s32[1]{0:T(128)} %bitcast.core_ref, bf16[4,2048,256]{2,1,0:T(8,128)(2,1)S(1)} %copy-done.3, bf16[2048,1024]{1,0:T(8,128)(2,1)S(1)} %copy-done.1, bf16[2048,1024]{1,0:T(8,128)(2,1)S(1)} %copy-done.5, bf16[2048,512]{1,0:T(8,128)(2,1)S(1)} %get-tuple-element.16.grad), custom_call_target="tpu_custom_call" | custom-call | flops 3200000000 | bytes 2097152 | tf_op jit(solution)/shard_map/mine_of/pallas_call | solution.py:263
  37.1 0.0 collective-permute-done.arrived
  37.2 3.0 %join_halves.1 = bf16[512,1536]{1,0:T(8,128)(2,1)} custom-call(f32[512,1536]{1,0:T(8,128)S(1)} %mine_of.1.mine, bf16[512,1536]{1,0:T(8,128)(2,1)} %collective-permute-done.arrived), custom_call_target="tpu_custom_call" | custom-call | flops 1000000 | bytes 2097152 | tf_op jit(solution)/shard_map/join_halves/pallas_call | solution.py:279
  40.1 0.5 all-to-all-done.1.own
  40.7 0.0 copy-start.6
  40.7 10.6 %all-to-all-start = ((bf16[64,8,1536]{2,1,0:T(8,128)(2,1)}), bf16[64,8,1536]{2,1,0:T(8,128)(2,1)S(1)}, u32[]{:S(2)}, u32[]{:S(2)}) async-start(bf16[64,8,1536]{2,1,0:T(8,128)(2,1)} %bitcast.1), calls=%async_computation | async-start | bytes 3145728 | tf_op jit(solution)/shard_map/all_to_all | solution.py:318
  51.3 0.0 copy-start.7
  51.3 0.1 collective-permute-start.1
  51.4 2.0 %collective-permute-done.1.other = bf16[32,72,128]{2,1,0:T(8,128)(2,1)S(1)} collective-permute-done((bf16[32,72,128]{2,1,0:T(8,128)(2,1)S(1)}, bf16[32,72,128]{2,1,0:T(8,128)(2,1)S(1)}, u32[]{:S(2)}, u32[]{:S(2)}) %collective-permute-start.1) | collective-permute-done | bytes 589856 | tf_op jit(solution)/shard_map/ppermute | solution.py:344
  53.4 2.3 %scatter_rows.1.near = bf16[1024,128]{1,0:T(8,128)(2,1)S(1)} custom-call(s32[1]{0:T(128)} %bitcast.core_ref, bf16[32,72,128]{2,1,0:T(8,128)(2,1)S(1)} %all-to-all-done.1.own, bf16[32,72,128]{2,1,0:T(8,128)(2,1)S(1)} %collective-permute-done.1.other), custom_call_target="tpu_custom_call" | custom-call | flops 1000000000 | bytes 1048576 | tf_op jit(solution)/shard_map/scatter_rows/pallas_call | solution.py:105
  55.8 3.3 %collective-permute-start.2 = (bf16[1024,128]{1,0:T(8,128)(2,1)S(1)}, bf16[1024,128]{1,0:T(8,128)(2,1)S(1)}, u32[]{:S(2)}, u32[]{:S(2)}) collective-permute-start(bf16[1024,128]{1,0:T(8,128)(2,1)S(1)} %scatter_rows.1.near), channel_id=1, source_target_pairs={{0,64},{64,0},{1,65},{65,1},{2,66},{66,2},{3,67},{67,3},{4,68},{68... | collective-permute-start | bytes 786440 | tf_op jit(solution)/shard_map/ppermute | solution.py:346
  59.0 0.0 collective-permute-start.3
  59.0 21.3 %collective-permute-done.2.far = bf16[1024,128]{1,0:T(8,128)(2,1)S(1)} collective-permute-done((bf16[1024,128]{1,0:T(8,128)(2,1)S(1)}, bf16[1024,128]{1,0:T(8,128)(2,1)S(1)}, u32[]{:S(2)}, u32[]{:S(2)}) %collective-permute-start.2) | collective-permute-done | bytes 262176 | tf_op jit(solution)/shard_map/ppermute | solution.py:346
  80.4 0.1 collective-permute-start.4
  80.4 0.0 collective-permute-done.3.near_other
  80.4 1.5 %collective-permute-done.4.far_other = bf16[1024,128]{1,0:T(8,128)(2,1)S(1)} collective-permute-done((bf16[1024,128]{1,0:T(8,128)(2,1)S(1)}, bf16[1024,128]{1,0:T(8,128)(2,1)S(1)}, u32[]{:S(2)}, u32[]{:S(2)}) %collective-permute-start.4) | collective-permute-done | bytes 262176 | tf_op jit(solution)/shard_map/ppermute | solution.py:348
  81.9 0.0 copy-done.6
  81.9 0.0 copy-done.7
  81.9 1.7 %update_rows.1 = (f32[2048,128]{1,0:T(8,128)}, f32[2048,128]{1,0:T(8,128)}) custom-call(s32[1]{0:T(128)} %bitcast.core_ref, bf16[1024,128]{1,0:T(8,128)(2,1)S(1)} %scatter_rows.1.near, bf16[1024,128]{1,0:T(8,128)(2,1)S(1)} %collective-permute-done.2.far, bf16[1024,128]{1,0:T(8,128)(2,1)S(1)} %collective-permute-done.3.near_other, ...), custom_call_target="tpu_custom_call" | custom-call | flops 2000000 | bytes 5242880 | tf_op jit(solution)/shard_map/update_rows/pallas_call | solution.py:132
  83.6 0.0 all-to-all-done.blocks
  83.6 0.9 %total_blocks.1 = (f32[8,1024]{1,0:T(8,128)}, f32[8,512]{1,0:T(8,128)}) custom-call(bf16[64,8,1536]{2,1,0:T(8,128)(2,1)S(1)} %all-to-all-done.blocks), custom_call_target="tpu_custom_call" | custom-call | flops 1000000 | bytes 2097152 | tf_op jit(solution)/shard_map/total_blocks/pallas_call | solution.py:301
Async XLA Ops:
  10.5 2.0 %copy-start = (bf16[2048,1024]{1,0:T(8,128)(2,1)}, bf16[2048,1024]{1,0:T(8,128)(2,1)S(1)}, u32[]{:S(2)}) copy-start(bf16[2048,1024]{1,0:T(8,128)(2,1)S(1)} %get-tuple-element.14.d_hidden) | copy-start | bytes 12582916
  12.5 2.0 %copy-start.2 = (bf16[4,2048,256]{2,1,0:T(8,128)(2,1)}, bf16[4,2048,256]{2,1,0:T(8,128)(2,1)S(1)}, u32[]{:S(2)}) copy-start(bf16[4,2048,256]{2,1,0:T(8,128)(2,1)S(1)} %get-tuple-element.13.given_kept) | copy-start | bytes 12582916
  14.4 2.0 %copy-start.4 = (bf16[2048,1024]{1,0:T(8,128)(2,1)}, bf16[2048,1024]{1,0:T(8,128)(2,1)S(1)}, u32[]{:S(2)}) copy-start(bf16[2048,1024]{1,0:T(8,128)(2,1)S(1)} %get-tuple-element.15.hidden_kept) | copy-start | bytes 12582916
  16.4 20.8 %collective-permute-start = (bf16[512,1536]{1,0:T(8,128)(2,1)}, bf16[512,1536]{1,0:T(8,128)(2,1)}, u32[]{:S(2)}, u32[]{:S(2)}) collective-permute-start(bf16[512,1536]{1,0:T(8,128)(2,1)} %get-tuple-element.17), channel_id=1, source_target_pairs={{0,32},{32,0},{1,33},{33,1},{2,34},{34,2},{3,35},{35,3},{4,36},{36... | collective-permute-start | bytes 4718600 | tf_op jit(solution)/shard_map/ppermute | solution.py:338
  18.3 22.4 %all-to-all-start.1 = ((bf16[32,72,128]{2,1,0:T(8,128)(2,1)}), bf16[32,72,128]{2,1,0:T(8,128)(2,1)S(1)}, u32[]{:S(2)}, u32[]{:S(2)}) async-start(bf16[32,72,128]{2,1,0:T(8,128)(2,1)} %pack_rows.1), calls=%async_computation.1 | async-start | bytes 1179648 | tf_op jit(solution)/shard_map/all_to_all | solution.py:333
  27.1 2.2 %copy-start.1 = (bf16[2048,1024]{1,0:T(8,128)(2,1)S(1)}, bf16[2048,1024]{1,0:T(8,128)(2,1)}, u32[]{:S(2)}) copy-start(bf16[2048,1024]{1,0:T(8,128)(2,1)} %copy-done) | copy-start | bytes 12582916
  29.3 2.2 %copy-start.3 = (bf16[4,2048,256]{2,1,0:T(8,128)(2,1)S(1)}, bf16[4,2048,256]{2,1,0:T(8,128)(2,1)}, u32[]{:S(2)}) copy-start(bf16[4,2048,256]{2,1,0:T(8,128)(2,1)} %copy-done.2) | copy-start | bytes 12582916
  31.5 2.2 %copy-start.5 = (bf16[2048,1024]{1,0:T(8,128)(2,1)S(1)}, bf16[2048,1024]{1,0:T(8,128)(2,1)}, u32[]{:S(2)}) copy-start(bf16[2048,1024]{1,0:T(8,128)(2,1)} %copy-done.4) | copy-start | bytes 12582916
  40.7 41.2 %copy-start.6 = (f32[2048,128]{1,0:T(8,128)S(1)}, f32[2048,128]{1,0:T(8,128)}, u32[]{:S(2)}) copy-start(f32[2048,128]{1,0:T(8,128)} %table.1) | copy-start | bytes 3145732
  40.7 42.9 %all-to-all-start = ((bf16[64,8,1536]{2,1,0:T(8,128)(2,1)}), bf16[64,8,1536]{2,1,0:T(8,128)(2,1)S(1)}, u32[]{:S(2)}, u32[]{:S(2)}) async-start(bf16[64,8,1536]{2,1,0:T(8,128)(2,1)} %bitcast.1), calls=%async_computation | async-start | bytes 3145728 | tf_op jit(solution)/shard_map/all_to_all | solution.py:318
  51.3 30.6 %copy-start.7 = (f32[2048,128]{1,0:T(8,128)S(1)}, f32[2048,128]{1,0:T(8,128)}, u32[]{:S(2)}) copy-start(f32[2048,128]{1,0:T(8,128)} %state.1) | copy-start | bytes 3145732
  51.3 2.1 %collective-permute-start.1 = (bf16[32,72,128]{2,1,0:T(8,128)(2,1)S(1)}, bf16[32,72,128]{2,1,0:T(8,128)(2,1)S(1)}, u32[]{:S(2)}, u32[]{:S(2)}) collective-permute-start(bf16[32,72,128]{2,1,0:T(8,128)(2,1)S(1)} %all-to-all-done.1.own), channel_id=1, source_target_pairs={{0,32},{32,0},{1,33},{33,1},{2,34},{34,2},{3,35},{35,3},{4,36},{36... | collective-permute-start | bytes 1769480 | tf_op jit(solution)/shard_map/ppermute | solution.py:344
  55.8 24.6 %collective-permute-start.2 = (bf16[1024,128]{1,0:T(8,128)(2,1)S(1)}, bf16[1024,128]{1,0:T(8,128)(2,1)S(1)}, u32[]{:S(2)}, u32[]{:S(2)}) collective-permute-start(bf16[1024,128]{1,0:T(8,128)(2,1)S(1)} %scatter_rows.1.near), channel_id=1, source_target_pairs={{0,64},{64,0},{1,65},{65,1},{2,66},{66,2},{3,67},{67,3},{4,68},{68... | collective-permute-start | bytes 786440 | tf_op jit(solution)/shard_map/ppermute | solution.py:346
  59.0 21.4 %collective-permute-start.3 = (bf16[1024,128]{1,0:T(8,128)(2,1)S(1)}, bf16[1024,128]{1,0:T(8,128)(2,1)S(1)}, u32[]{:S(2)}, u32[]{:S(2)}) collective-permute-start(bf16[1024,128]{1,0:T(8,128)(2,1)S(1)} %scatter_rows.1.near), channel_id=1, source_target_pairs={{0,32},{32,0},{1,33},{33,1},{2,34},{34,2},{3,35},{35,3},{4,36},{36... | collective-permute-start | bytes 786440 | tf_op jit(solution)/shard_map/ppermute | solution.py:347
  80.4 1.5 %collective-permute-start.4 = (bf16[1024,128]{1,0:T(8,128)(2,1)S(1)}, bf16[1024,128]{1,0:T(8,128)(2,1)S(1)}, u32[]{:S(2)}, u32[]{:S(2)}) collective-permute-start(bf16[1024,128]{1,0:T(8,128)(2,1)S(1)} %collective-permute-done.2.far), channel_id=1, source_target_pairs={{0,32},{32,0},{1,33},{33,1},{2,34},{34,2},{3,35},{35,3},{4,36},{36... | collective-permute-start | bytes 786440 | tf_op jit(solution)/shard_map/ppermute | solution.py:348

commit v2 on v1

--- a/solution.py
+++ b/solution.py
@@ -104,43 +104,43 @@
 def scattered(core, own, other, rows):
     return pl.pallas_call(
         scatter_kernel,
-        out_shape=jax.ShapeDtypeStruct((rows, own.shape[2]), jnp.bfloat16),
+        out_shape=pltpu.VMEM((rows, own.shape[2]), jnp.float32),
         in_specs=[IN_SMEM, IN_VMEM, IN_VMEM],
         out_specs=IN_VMEM,
         scratch_shapes=[pltpu.VMEM((rows, own.shape[2]), jnp.float32)],
         compiler_params=pltpu.CompilerParams(vmem_limit_bytes=16 << 20),
         cost_estimate=pl.CostEstimate(flops=1000000000, transcendentals=0, bytes_accessed=1 << 20),
         name="scatter_rows",
-    )(core, own, other)
-
-
-def update_kernel(core_ref, near, far, near_other, far_other, table, state, new_table, new_state):
-    half = near.shape[0]
-
-    def apply(place, first, second):
+    )(core, in_vmem(own), in_vmem(other))
+
+
+def update_kernel(core_ref, total, total_other, table, state, new_table, new_state):
+    half = total.shape[0]
+
+    def apply(place, grads):
         rows = pl.ds(pl.multiple_of(place * half, half), half)
-        grad = first[...].astype(jnp.float32) + second[...].astype(jnp.float32)
+        grad = grads[...]
         summed = state[rows, :] + grad * grad
         new_state[rows, :] = summed
         new_table[rows, :] = table[rows, :] - learn_rate * grad / (jnp.sqrt(summed) + epsilon)
 
-    apply(core_ref[0], near, far)
-    apply(1 - core_ref[0], near_other, far_other)
-
-
-def updated(core, near, far, near_other, far_other, table, state):
+    apply(core_ref[0], total)
+    apply(1 - core_ref[0], total_other)
+
+
+def updated(core, total, total_other, table, state):
     return pl.pallas_call(
         update_kernel,
         out_shape=(
             jax.ShapeDtypeStruct(table.shape, table.dtype),
             jax.ShapeDtypeStruct(state.shape, state.dtype),
         ),
-        in_specs=[IN_SMEM] + [IN_VMEM] * 6,
+        in_specs=[IN_SMEM] + [IN_VMEM] * 4,
         out_specs=(IN_VMEM, IN_VMEM),
         compiler_params=pltpu.CompilerParams(vmem_limit_bytes=16 << 20),
         cost_estimate=pl.CostEstimate(flops=2000000, transcendentals=0, bytes_accessed=5 << 20),
         name="update_rows",
-    )(core, near, far, near_other, far_other, table, state)
+    )(core, total, total_other, table, state)
 
 
 def columns_at(tile, core):
@@ -343,12 +343,11 @@
 
     other = lax.ppermute(own, "c", SWAP)
     near = scattered(at_core, own, other, emb_table.shape[0] // 2)
+    near = lax.optimization_barrier(near.astype(jnp.float16))
     far = lax.ppermute(near, "zh", SWAP)
-    near_other = lax.ppermute(near, "c", SWAP)
-    far_other = lax.ppermute(far, "c", SWAP)
-    new_table, new_state = updated(
-        at_core, near, far, near_other, far_other, emb_table, adagrad_state
-    )
+    total = near.astype(jnp.float32) + far.astype(jnp.float32)
+    total_other = lax.ppermute(total, "c", SWAP)
+    new_table, new_state = updated(at_core, total, total_other, emb_table, adagrad_state)
     return (grad_first, grad_second, new_table, new_state)
 
 

time: 86 us -> 80 us (0.930)
  blocking collectives: 0 us -> 22.2 us
  local copies, waits for them, and re-layouts: 12.5 us -> 0.01 us
  starting transfers between devices: 22.8 us -> 10.6 us
  Pallas kernels: 23.1 us -> 19.5 us
    all_to_all x0 -> x1, blocking collectives: none -> 22.2 us  [on_device(): lax.all_to_all(packed(block_counts, row_ids, row_grads), DEV, 0, 0, tiled...]
    unnamed x16 -> x4, local copies, waits for them, and re-layouts: 12.5 us -> 0.01 us
    all_to_all x1 -> x0, starting transfers between devices: 8.79 us -> none  [on_device(): lax.all_to_all(packed(block_counts, row_ids, row_grads), DEV, 0, 0, tiled...]
    all_to_all x1, starting transfers between devices: 10.6 us -> 7.19 us  [to_owners(): return lax.all_to_all(blocks, CHIPS, 0, 0, tiled=True)]
    ppermute x1, waiting for transfers between devices: 21.3 us -> 23.7 us  [on_device(): far = lax.ppermute(near, 'zh', SWAP)]
    ppermute x1, waiting for transfers between devices: 1.99 us -> 0.01 us  [on_device(): other = lax.ppermute(own, 'c', SWAP)]
    pallas_call x1, Pallas kernels: 2.99 us -> 1.41 us  [joined(): pl.pallas_call(join_kernel, out_shape=pltpu.VMEM(mine.shape, jnp.bfloat16...]
    pallas_call x1, Pallas kernels: 9.82 us -> 8.72 us  [theirs_of(): pl.pallas_call(theirs_kernel, out_shape=(pltpu.VMEM(hidden.shape, jnp.bfl...]
  transfers between devices with their start and end apart: 7 -> 5, of which waited for: 4 -> 2; matrix products, arithmetic and copies ran while one was open for 0% -> 0% of each run, Pallas kernels for 15% -> 13%
where the time goes in v2:
time: 80 us; the launch traced here: 78.7 us
  waiting for transfers between devices  25.6 us (32%)
  blocking collectives  22.2 us (28%)
  Pallas kernels  19.5 us (24%)
  starting transfers between devices  10.6 us (13%)
    ppermute x1, waiting for transfers between devices, on_device(): far = lax.ppermute(near, 'zh', SWAP)  23.7 us
    all_to_all x1, blocking collectives, on_device(): lax.all_to_all(packed(block_counts, row_ids, row_grads), DEV, 0, 0, tiled...  22.2 us
    pallas_call x1, Pallas kernels, theirs_of(): pl.pallas_call(theirs_kernel, out_shape=(pltpu.VMEM(hidden.shape, jnp.bfl...  8.72 us
    all_to_all x1, starting transfers between devices, to_owners(): return lax.all_to_all(blocks, CHIPS, 0, 0, tiled=True)  7.19 us
    pallas_call x1, Pallas kernels, mine_of(): pl.pallas_call(mine_kernel, out_shape=pltpu.VMEM((2 * WIDTH, columns), jn...  3.45 us
    ppermute x1, starting transfers between devices, on_device(): far = lax.ppermute(near, 'zh', SWAP)  3.25 us
    pallas_call x1, Pallas kernels, scattered(): pl.pallas_call(scatter_kernel, out_shape=pltpu.VMEM((rows, own.shape[2]),...  2.32 us
    ppermute x1, waiting for transfers between devices, on_device(): total_other = lax.ppermute(total, 'c', SWAP)  1.9 us
  transfers between devices with their start and end apart: 5, of which 2 were waited for; matrix products, arithmetic and copies ran while one was open for 0% of the time, Pallas kernels for 13%

profile of v2, /device:TPU:0, one launch (start us, length us, event | category | flops | bytes accessed | tf_op | source)
XLA Modules:
  0.0 78.7 jit_solution(7155206885853017606)
XLA Ops:
  0.6 8.7 %theirs_of.1 = (bf16[2048,1024]{1,0:T(8,128)(2,1)S(1)}, bf16[512,1536]{1,0:T(8,128)(2,1)S(1)}, bf16[2048,512]{1,0:T(8,128)(2,1)S(1)}, bf16[4,2048,256]{2,1,0:T(8,128)(2,1)S(1)}, bf16[2048,1024]{1,0:T(8,128)(2,1)S(1)}) custom-call(s32[1]{0:T(128)} %bitcast.core_ref, bf16[2048,512]{1,0:T(8,128)(2,1)} %grad.1, bf16[1024,512]{1,0:T(8,128)(2,1)} %weight.1, ...), custom_call_target="tpu_custom_call" | custom-call | flops 5400000000 | bytes 11534336 | tf_op jit(solution)/shard_map/theirs_of/pallas_call | solution.py:237
  9.4 0.1 collective-permute-start
  9.5 1.1 %pack_rows.1 = bf16[32,72,128]{2,1,0:T(8,128)(2,1)S(1)} custom-call(s32[32]{0:T(128)} %counts_from.1, s32[16,128]{1,0:T(8,128)} %bitcast.5, bf16[32,64,128]{2,1,0:T(8,128)(2,1)} %bitcast.4), custom_call_target="tpu_custom_call" | custom-call | flops 1000000 | bytes 1048576 | tf_op jit(solution)/shard_map/pack_rows/pallas_call | solution.py:59
  10.6 22.2 %all_to_all.10.own = bf16[32,72,128]{2,1,0:T(8,128)(2,1)S(1)} all-to-all(bf16[32,72,128]{2,1,0:T(8,128)(2,1)S(1)} %pack_rows.1), channel_id=1, replica_groups=mesh['zh'=2,'c'=2,'y'=4,'x'=4,'zl'=2] {'y','x','zl'}, dimensions={0} | all-to-all | bytes 1179648 | tf_op jit(solution)/shard_map/all_to_all | solution.py:333
  32.7 0.0 collective-permute-start.1
  32.7 3.5 %mine_of.1.mine = f32[512,1536]{1,0:T(8,128)S(1)} custom-call(s32[1]{0:T(128)} %bitcast.core_ref, bf16[4,2048,256]{2,1,0:T(8,128)(2,1)S(1)} %get-tuple-element.13.given_kept, bf16[2048,1024]{1,0:T(8,128)(2,1)S(1)} %get-tuple-element.14.d_hidden, bf16[2048,1024]{1,0:T(8,128)(2,1)S(1)} %get-tuple-element.15.hidden_kept, ...), custom_call_target="tpu_custom_call" | custom-call | flops 3200000000 | bytes 2097152 | tf_op jit(solution)/shard_map/mine_of/pallas_call | solution.py:263
  36.2 0.0 collective-permute-done.arrived
  36.2 1.4 %join_halves.1 = bf16[512,1536]{1,0:T(8,128)(2,1)} custom-call(f32[512,1536]{1,0:T(8,128)S(1)} %mine_of.1.mine, bf16[512,1536]{1,0:T(8,128)(2,1)S(1)} %collective-permute-done.arrived), custom_call_target="tpu_custom_call" | custom-call | flops 1000000 | bytes 2097152 | tf_op jit(solution)/shard_map/join_halves/pallas_call | solution.py:279
  37.6 7.2 %all-to-all-start = ((bf16[64,8,1536]{2,1,0:T(8,128)(2,1)}), bf16[64,8,1536]{2,1,0:T(8,128)(2,1)S(1)}, u32[]{:S(2)}, u32[]{:S(2)}) async-start(bf16[64,8,1536]{2,1,0:T(8,128)(2,1)} %bitcast.1), calls=%async_computation | async-start | bytes 3145728 | tf_op jit(solution)/shard_map/all_to_all | solution.py:318
  44.8 0.0 copy-start
  44.8 0.0 copy-start.1
  44.8 0.0 collective-permute-done.1.other
  44.8 2.3 %scatter_rows.1 = f32[1024,128]{1,0:T(8,128)S(1)} custom-call(s32[1]{0:T(128)} %bitcast.core_ref, bf16[32,72,128]{2,1,0:T(8,128)(2,1)S(1)} %all_to_all.10.own, bf16[32,72,128]{2,1,0:T(8,128)(2,1)S(1)} %collective-permute-done.1.other), custom_call_target="tpu_custom_call" | custom-call | flops 1000000000 | bytes 1048576 | tf_op jit(solution)/shard_map/scatter_rows/pallas_call | solution.py:105
  47.2 3.3 %collective-permute-start.2 = (f16[1024,128]{1,0:T(8,128)(2,1)S(1)}, f16[1024,128]{1,0:T(8,128)(2,1)S(1)}, u32[]{:S(2)}, u32[]{:S(2)}) collective-permute-start(f16[1024,128]{1,0:T(8,128)(2,1)S(1)} %convert_element_type.9), channel_id=1, source_target_pairs={{0,64},{64,0},{1,65},{65,1},{2,66},{66,2},{3,67},{67,3},{4,68},{68... | collective-permute-start | bytes 786440 | tf_op jit(solution)/shard_map/ppermute | solution.py:347
  50.5 23.7 %collective-permute-done.2 = f16[1024,128]{1,0:T(8,128)(2,1)S(1)} collective-permute-done((f16[1024,128]{1,0:T(8,128)(2,1)S(1)}, f16[1024,128]{1,0:T(8,128)(2,1)S(1)}, u32[]{:S(2)}, u32[]{:S(2)}) %collective-permute-start.2) | collective-permute-done | bytes 262176 | tf_op jit(solution)/shard_map/ppermute | solution.py:347
  74.1 0.1 convert_add_fusion.total
  74.2 0.1 collective-permute-start.3
  74.3 1.9 %collective-permute-done.3.total_other = f32[1024,128]{1,0:T(8,128)S(1)} collective-permute-done((f32[1024,128]{1,0:T(8,128)S(1)}, f32[1024,128]{1,0:T(8,128)S(1)}, u32[]{:S(2)}, u32[]{:S(2)}) %collective-permute-start.3) | collective-permute-done | bytes 524320 | tf_op jit(solution)/shard_map/ppermute | solution.py:349
  76.2 0.0 copy-done
  76.2 0.0 copy-done.1
  76.2 1.6 %update_rows.1 = (f32[2048,128]{1,0:T(8,128)}, f32[2048,128]{1,0:T(8,128)}) custom-call(s32[1]{0:T(128)} %bitcast.core_ref, f32[1024,128]{1,0:T(8,128)S(1)} %convert_add_fusion.total, f32[1024,128]{1,0:T(8,128)S(1)} %collective-permute-done.3.total_other, f32[2048,128]{1,0:T(8,128)S(1)} %copy-done, f32[2048,128]{1,0:T(8,128)S(1)} %copy-done.1), custom_call_target="tpu_custom_call" | custom-call | flops 2000000 | bytes 5242880 | tf_op jit(solution)/shard_map/update_rows/pallas_call | solution.py:132
  77.8 0.0 all-to-all-done.blocks
  77.8 0.9 %total_blocks.1 = (f32[8,1024]{1,0:T(8,128)}, f32[8,512]{1,0:T(8,128)}) custom-call(bf16[64,8,1536]{2,1,0:T(8,128)(2,1)S(1)} %all-to-all-done.blocks), custom_call_target="tpu_custom_call" | custom-call | flops 1000000 | bytes 2097152 | tf_op jit(solution)/shard_map/total_blocks/pallas_call | solution.py:301
  (1 shorter events, 0.0 us)
Async XLA Ops:
  9.4 26.8 %collective-permute-start = (bf16[512,1536]{1,0:T(8,128)(2,1)S(1)}, bf16[512,1536]{1,0:T(8,128)(2,1)S(1)}, u32[]{:S(2)}, u32[]{:S(2)}) collective-permute-start(bf16[512,1536]{1,0:T(8,128)(2,1)S(1)} %get-tuple-element.17), channel_id=1, source_target_pairs={{0,32},{32,0},{1,33},{33,1},{2,34},{34,2},{3,35},{35,3},{4,36},{36... | collective-permute-start | bytes 4718600 | tf_op jit(solution)/shard_map/ppermute | solution.py:338
  32.7 12.1 %collective-permute-start.1 = (bf16[32,72,128]{2,1,0:T(8,128)(2,1)S(1)}, bf16[32,72,128]{2,1,0:T(8,128)(2,1)S(1)}, u32[]{:S(2)}, u32[]{:S(2)}) collective-permute-start(bf16[32,72,128]{2,1,0:T(8,128)(2,1)S(1)} %all_to_all.10.own), channel_id=1, source_target_pairs={{0,32},{32,0},{1,33},{33,1},{2,34},{34,2},{3,35},{35,3},{4,36},{36... | collective-permute-start | bytes 1769480 | tf_op jit(solution)/shard_map/ppermute | solution.py:344
  37.6 40.2 %all-to-all-start = ((bf16[64,8,1536]{2,1,0:T(8,128)(2,1)}), bf16[64,8,1536]{2,1,0:T(8,128)(2,1)S(1)}, u32[]{:S(2)}, u32[]{:S(2)}) async-start(bf16[64,8,1536]{2,1,0:T(8,128)(2,1)} %bitcast.1), calls=%async_computation | async-start | bytes 3145728 | tf_op jit(solution)/shard_map/all_to_all | solution.py:318
  44.8 31.4 %copy-start = (f32[2048,128]{1,0:T(8,128)S(1)}, f32[2048,128]{1,0:T(8,128)}, u32[]{:S(2)}) copy-start(f32[2048,128]{1,0:T(8,128)} %table.1) | copy-start | bytes 3145732
  44.8 31.4 %copy-start.1 = (f32[2048,128]{1,0:T(8,128)S(1)}, f32[2048,128]{1,0:T(8,128)}, u32[]{:S(2)}) copy-start(f32[2048,128]{1,0:T(8,128)} %state.1) | copy-start | bytes 3145732
  47.2 26.9 %collective-permute-start.2 = (f16[1024,128]{1,0:T(8,128)(2,1)S(1)}, f16[1024,128]{1,0:T(8,128)(2,1)S(1)}, u32[]{:S(2)}, u32[]{:S(2)}) collective-permute-start(f16[1024,128]{1,0:T(8,128)(2,1)S(1)} %convert_element_type.9), channel_id=1, source_target_pairs={{0,64},{64,0},{1,65},{65,1},{2,66},{66,2},{3,67},{67,3},{4,68},{68... | collective-permute-start | bytes 786440 | tf_op jit(solution)/shard_map/ppermute | solution.py:347
  74.2 2.0 %collective-permute-start.3 = (f32[1024,128]{1,0:T(8,128)S(1)}, f32[1024,128]{1,0:T(8,128)S(1)}, u32[]{:S(2)}, u32[]{:S(2)}) collective-permute-start(f32[1024,128]{1,0:T(8,128)S(1)} %convert_add_fusion.total), channel_id=1, source_target_pairs={{0,32},{32,0},{1,33},{33,1},{2,34},{34,2},{3,35},{35,3},{4,36},{36... | collective-permute-start | bytes 1572872 | tf_op jit(solution)/shard_map/ppermute | solution.py:349

commit v3 on v2

--- a/solution.py
+++ b/solution.py
@@ -27,29 +27,37 @@
     return pltpu.with_memory_space_constraint(array, pltpu.HBM)
 
 
-def pack_kernel(counts_from, ids_from, grads, out, counts, ids, sems):
+def pack_kernel(counts_from, ids_from, grads, out, counts, ids, kept, tails, sems):
     blocks, height = out.shape[:2]
     capacity = height - 8
     counts_copy = pltpu.make_async_copy(counts_from, counts, sems.at[0])
     ids_copy = pltpu.make_async_copy(ids_from, ids, sems.at[1])
-    grads_copy = pltpu.make_async_copy(grads, out.at[:, pl.ds(0, capacity), :], sems.at[2])
-    counts_copy.start()
-    ids_copy.start()
-    grads_copy.start()
+    grads_copy = pltpu.make_async_copy(grads, kept, sems.at[2])
+    grads_out = pltpu.make_async_copy(kept, out.at[:, pl.ds(0, capacity), :], sems.at[3])
+    tails_out = pltpu.make_async_copy(tails, out.at[:, pl.ds(capacity, 8), :], sems.at[4])
+    copy_all([counts_copy, ids_copy, grads_copy])
     lane = lax.broadcasted_iota(jnp.int32, (1, 128), 1)
     row = lax.broadcasted_iota(jnp.int32, (8, 128), 0)
+    grads_copy.wait()
+    grads_out.start()
     counts_copy.wait()
     ids_copy.wait()
+    here = ids[...]
+    turned = pltpu.roll(here, capacity, 1)
     for block in range(blocks):
-        here = ids[pl.ds(block // 2, 1), :]
-        turned = pltpu.roll(here, capacity, 1)
-        twice = jnp.where((lane < capacity) == (block % 2 == 0), here, turned)
+        pair = block // 2
+        left = lane < capacity
+        twice = jnp.where(
+            left == (block % 2 == 0), here[pair : pair + 1], turned[pair : pair + 1]
+        )
         usable = lax.rem(lane, capacity) < counts[block]
         high = jnp.where(usable, lax.shift_right_logical(twice, 6), 2 * LOW)
         low = jnp.where(usable, lax.bitwise_and(twice, LOW - 1), 0)
         tail = jnp.where(row == 0, high, jnp.where(row == 1, low, 0))
-        out[block, pl.ds(capacity, 8), :] = tail.astype(jnp.float32).astype(out.dtype)
-    grads_copy.wait()
+        tails[block] = tail.astype(jnp.float32).astype(out.dtype)
+    tails_out.start()
+    grads_out.wait()
+    tails_out.wait()
 
 
 def packed(counts, ids, grads):
@@ -58,13 +66,15 @@
     ids = ids.reshape(-1, 128)
     return pl.pallas_call(
         pack_kernel,
-        out_shape=pltpu.VMEM((blocks, capacity + 8, width), grads.dtype),
+        out_shape=pltpu.HBM((blocks, capacity + 8, width), grads.dtype),
         in_specs=[IN_HBM] * 3,
-        out_specs=IN_VMEM,
+        out_specs=IN_HBM,
         scratch_shapes=[
             pltpu.SMEM((blocks,), jnp.int32),
             pltpu.VMEM(ids.shape, jnp.int32),
-            pltpu.SemaphoreType.DMA((3,)),
+            pltpu.VMEM((blocks, capacity, width), grads.dtype),
+            pltpu.VMEM((blocks, 8, width), grads.dtype),
+            pltpu.SemaphoreType.DMA((5,)),
         ],
         compiler_params=pltpu.CompilerParams(vmem_limit_bytes=8 << 20),
         cost_estimate=pl.CostEstimate(flops=1000000, transcendentals=0, bytes_accessed=1 << 20),
@@ -72,57 +82,66 @@
     )(in_hbm(counts), in_hbm(ids), in_hbm(grads.reshape(blocks, capacity, width)))
 
 
-def scatter_kernel(core_ref, own, other, out, acc):
-    rows = acc.shape[0]
+def scatter_into(core_ref, blocks, acc, out):
+    rows = out.shape[0]
     wanted = core_ref[0] * rows + lax.broadcasted_iota(jnp.int32, (rows, 128), 0)
     lane = lax.broadcasted_iota(jnp.int32, (1, 128), 1)
 
-    def ids_of(blocks, block):
+    def ids_of(block):
         tail = blocks[block, pl.ds(64, 8), :].astype(jnp.float32)
         return (tail[0:1] * LOW + tail[1:2]).astype(jnp.int32)
 
-    first = True
-    for blocks in (own, other):
-        for step in range(blocks.shape[0] // 4):
-            hot = []
-            for block in (4 * step, 4 * step + 2):
-                ids = jnp.where(lane < 64, ids_of(blocks, block), ids_of(blocks, block + 1))
-                same = wanted == jnp.broadcast_to(ids, (rows, 128))
-                hot.append(same.astype(jnp.float32).astype(jnp.bfloat16))
-            values = blocks[pl.ds(4 * step, 4), pl.ds(0, 64), :].reshape(256, 128)
-            part = jnp.dot(
-                jnp.concatenate(hot, axis=1), values, preferred_element_type=jnp.float32
+    total = None if acc is None else acc[...]
+    for step in range(blocks.shape[0] // 4):
+        hot = []
+        for block in (4 * step, 4 * step + 2):
+            ids = jnp.where(lane < 64, ids_of(block), ids_of(block + 1))
+            same = wanted == jnp.broadcast_to(ids, (rows, 128))
+            hot.append(same.astype(jnp.float32).astype(jnp.bfloat16))
+        values = blocks[pl.ds(4 * step, 4), pl.ds(0, 64), :].reshape(256, 128)
+        part = jnp.dot(jnp.concatenate(hot, axis=1), values, preferred_element_type=jnp.float32)
+        out[...] = part if total is None else total + part
+        total = out[...]
+
+
+def scatter_own_kernel(core_ref, blocks, out):
+    scatter_into(core_ref, blocks, None, out)
+
+
+def scatter_other_kernel(core_ref, blocks, acc, out):
+    scatter_into(core_ref, blocks, acc, out)
+
+
+def scattered(kernel, core, rows, blocks, *acc):
+    return pl.pallas_call(
+        kernel,
+        out_shape=pltpu.VMEM((rows, blocks.shape[2]), jnp.float32),
+        in_specs=[IN_SMEM] + [IN_VMEM] * (1 + len(acc)),
+        out_specs=IN_VMEM,
+        compiler_params=pltpu.CompilerParams(vmem_limit_bytes=16 << 20),
+        cost_estimate=pl.CostEstimate(flops=500000000, transcendentals=0, bytes_accessed=1 << 20),
+    )(core, in_vmem(blocks), *acc)
+
+
+def update_kernel(core_ref, total, total_other, table, state, new_table, new_state, kept, sems):
+    half = total.shape[0]
+    copies = []
+    for i, source in enumerate((table, state)):
+        for part in range(2):
+            rows = pl.ds(part * half, half)
+            copies.append(
+                pltpu.make_async_copy(source.at[rows, :], kept.at[i, rows, :], sems.at[i, part])
             )
-            if first:
-                acc[...] = part
-                first = False
-            else:
-                acc[...] += part
-    out[...] = acc[...].astype(out.dtype)
-
-
-def scattered(core, own, other, rows):
-    return pl.pallas_call(
-        scatter_kernel,
-        out_shape=pltpu.VMEM((rows, own.shape[2]), jnp.float32),
-        in_specs=[IN_SMEM, IN_VMEM, IN_VMEM],
-        out_specs=IN_VMEM,
-        scratch_shapes=[pltpu.VMEM((rows, own.shape[2]), jnp.float32)],
-        compiler_params=pltpu.CompilerParams(vmem_limit_bytes=16 << 20),
-        cost_estimate=pl.CostEstimate(flops=1000000000, transcendentals=0, bytes_accessed=1 << 20),
-        name="scatter_rows",
-    )(core, in_vmem(own), in_vmem(other))
-
-
-def update_kernel(core_ref, total, total_other, table, state, new_table, new_state):
-    half = total.shape[0]
+    copy_all(copies)
+    for copy in copies:
+        copy.wait()
 
     def apply(place, grads):
         rows = pl.ds(pl.multiple_of(place * half, half), half)
         grad = grads[...]
-        summed = state[rows, :] + grad * grad
+        summed = kept[1, rows, :] + grad * grad
         new_state[rows, :] = summed
-        new_table[rows, :] = table[rows, :] - learn_rate * grad / (jnp.sqrt(summed) + epsilon)
+        new_table[rows, :] = kept[0, rows, :] - learn_rate * grad / (jnp.sqrt(summed) + epsilon)
 
     apply(core_ref[0], total)
     apply(1 - core_ref[0], total_other)
@@ -135,12 +154,21 @@
             jax.ShapeDtypeStruct(table.shape, table.dtype),
             jax.ShapeDtypeStruct(state.shape, state.dtype),
         ),
-        in_specs=[IN_SMEM] + [IN_VMEM] * 4,
+        in_specs=[IN_SMEM, IN_VMEM, IN_VMEM, IN_HBM, IN_HBM],
         out_specs=(IN_VMEM, IN_VMEM),
+        scratch_shapes=[
+            pltpu.VMEM((2,) + table.shape, table.dtype),
+            pltpu.SemaphoreType.DMA((2, 2)),
+        ],
         compiler_params=pltpu.CompilerParams(vmem_limit_bytes=16 << 20),
         cost_estimate=pl.CostEstimate(flops=2000000, transcendentals=0, bytes_accessed=5 << 20),
         name="update_rows",
-    )(core, total, total_other, table, state)
+    )(core, total, total_other, in_hbm(table), in_hbm(state))
+
+
+def copy_all(copies):
+    for copy in copies:
+        copy.start()
 
 
 def columns_at(tile, core):
@@ -152,7 +180,7 @@
     return [
         pltpu.make_async_copy(
             source.at[:, columns_at(tile, of)],
-            kept.at[place],
+            kept.at[place // 2, :, pl.ds(place % 2 * WIDTH, WIDTH)],
             sems.at[place],
         )
         for place, (tile, of) in enumerate(wanted)
@@ -163,7 +191,8 @@
     return lax.dot_general(left, right, ROWS_CONTRACTED, preferred_element_type=jnp.float32)
 
 
-def active_of(pre):
+def active_of(hidden, core):
+    pre = jnp.concatenate([hidden[:, columns_at(tile, core)] for tile in range(2)], axis=1)
     return jnp.maximum(pre, jnp.zeros((), pre.dtype))
 
 
@@ -172,13 +201,14 @@
     weight_kept, weight_sem, grad_sems, hidden_sems, given_sems,
 ):
     steps = grad_sems.shape[0]
-    height = grad.shape[0] // steps
+    unit = grad.shape[0] // 8
+    begins = (0, 2, 4, 6, 8)
     core = core_ref[0]
     wide = d_out.shape[1]
     weight_copy = pltpu.make_async_copy(weight, weight_kept, weight_sem)
 
     def part(source, kept, sems, i):
-        rows = pl.ds(i * height, height)
+        rows = pl.ds(begins[i] * unit, (begins[i + 1] - begins[i]) * unit)
         return pltpu.make_async_copy(source.at[rows, :], kept.at[rows, :], sems.at[i])
 
     given_copies = column_tiles(given, given_kept, given_sems, core)
@@ -192,7 +222,7 @@
     start_part(1)
     weight_copy.wait()
     for i in range(steps):
-        rows = pl.ds(i * height, height)
+        rows = pl.ds(begins[i] * unit, (begins[i + 1] - begins[i]) * unit)
         part(grad, grad_kept, grad_sems, i).wait()
         part(hidden, hidden_kept, hidden_sems, i).wait()
         if i + 2 < steps:
@@ -205,30 +235,22 @@
         )
         d_out[rows, :] = jnp.where(hidden_kept[rows, :] > 0, back, 0.0).astype(d_out.dtype)
 
-    for place in range(2):
-        rows = pl.ds(place * WIDTH, WIDTH)
-        given_copies[place].wait()
-        theirs[rows, pl.ds(0, wide)] = transposed_dot(given_kept[place], d_out[...]).astype(
-            theirs.dtype
-        )
-    for place in range(2):
-        rows = pl.ds(place * WIDTH, WIDTH)
-        theirs[rows, pl.ds(wide, grad.shape[1])] = transposed_dot(
-            active_of(hidden_kept[:, columns_at(place, 1 - core)]), grad_kept[...]
-        ).astype(theirs.dtype)
+    given_copies[0].wait()
+    given_copies[1].wait()
+    theirs[:, pl.ds(0, wide)] = transposed_dot(given_kept[0], d_out[...]).astype(theirs.dtype)
+    theirs[:, pl.ds(wide, grad.shape[1])] = transposed_dot(
+        active_of(hidden_kept, 1 - core), grad_kept[...]
+    ).astype(theirs.dtype)
     for copy in given_copies[2:]:
         copy.wait()
 
 
 def mine_kernel(core_ref, given_kept, d_hidden, hidden_kept, grad, mine):
-    core = core_ref[0]
     wide = d_hidden.shape[1]
-    for place in range(2):
-        rows = pl.ds(place * WIDTH, WIDTH)
-        mine[rows, pl.ds(0, wide)] = transposed_dot(given_kept[2 + place], d_hidden[...])
-        mine[rows, pl.ds(wide, grad.shape[1])] = transposed_dot(
-            active_of(hidden_kept[:, columns_at(place, core)]), grad[...]
-        )
+    mine[:, pl.ds(0, wide)] = transposed_dot(given_kept[1], d_hidden[...])
+    mine[:, pl.ds(wide, grad.shape[1])] = transposed_dot(
+        active_of(hidden_kept, core_ref[0]), grad[...]
+    )
 
 
 def theirs_of(core, grad, weight, hidden, given):
@@ -240,7 +262,7 @@
             pltpu.VMEM(hidden.shape, jnp.bfloat16),
             pltpu.VMEM((2 * WIDTH, columns), jnp.bfloat16),
             pltpu.VMEM(grad.shape, grad.dtype),
-            pltpu.VMEM((4, tokens, WIDTH), given.dtype),
+            pltpu.VMEM((2, tokens, 2 * WIDTH), given.dtype),
             pltpu.VMEM(hidden.shape, hidden.dtype),
         ),
         in_specs=[IN_SMEM] + [IN_HBM] * 4,
@@ -271,16 +293,26 @@
     )(core, in_vmem(given), in_vmem(d_hidden), in_vmem(hidden), in_vmem(grad))
 
 
-def join_kernel(mine, arrived, out):
-    out[...] = (mine[...] + arrived[...].astype(jnp.float32)).astype(out.dtype)
+def join_kernel(mine, arrived, out, kept, sems):
+    parts = sems.shape[0]
+    height = mine.shape[0] // parts
+    copies = []
+    for part in range(parts):
+        rows = pl.ds(part * height, height)
+        kept[rows, :] = (mine[rows, :] + arrived[rows, :].astype(jnp.float32)).astype(kept.dtype)
+        copies.append(pltpu.make_async_copy(kept.at[rows, :], out.at[rows, :], sems.at[part]))
+        copies[-1].start()
+    for copy in copies:
+        copy.wait()
 
 
 def joined(mine, arrived):
     return pl.pallas_call(
         join_kernel,
-        out_shape=pltpu.VMEM(mine.shape, jnp.bfloat16),
+        out_shape=pltpu.HBM(mine.shape, jnp.bfloat16),
         in_specs=[IN_VMEM, IN_VMEM],
-        out_specs=IN_VMEM,
+        out_specs=IN_HBM,
+        scratch_shapes=[pltpu.VMEM(mine.shape, jnp.bfloat16), pltpu.SemaphoreType.DMA((4,))],
         compiler_params=pltpu.CompilerParams(vmem_limit_bytes=16 << 20),
         cost_estimate=pl.CostEstimate(flops=1000000, transcendentals=0, bytes_accessed=2 << 20),
         name="join_halves",
@@ -330,7 +362,8 @@
     adagrad_state,
 ):
     at_core = lax.axis_index("c").astype(jnp.int32).reshape(1)
-    own = lax.all_to_all(packed(block_counts, row_ids, row_grads), DEV, 0, 0, tiled=True)
+    message = packed(block_counts, row_ids, row_grads)
+    own = lax.all_to_all(message, DEV, 0, 0, tiled=True)
 
     d_hidden, theirs, grad_kept, given_kept, hidden_kept = theirs_of(
         at_core, out_grad, second_weight, hidden_pre, layer_input
@@ -342,7 +375,9 @@
     grad_first, grad_second = totals(blocks, hidden_pre.shape[1])
 
     other = lax.ppermute(own, "c", SWAP)
-    near = scattered(at_core, own, other, emb_table.shape[0] // 2)
+    half = emb_table.shape[0] // 2
+    near = scattered(scatter_own_kernel, at_core, half, own)
+    near = scattered(scatter_other_kernel, at_core, half, other, near)
     near = lax.optimization_barrier(near.astype(jnp.float16))
     far = lax.ppermute(near, "zh", SWAP)
     total = near.astype(jnp.float32) + far.astype(jnp.float32)

time: 80 us -> 82.2 us (1.028)
  Pallas kernels: 19.5 us -> 21.5 us
    pallas_call x1, Pallas kernels: 1.64 us -> 3.17 us  [updated(): pl.pallas_call(update_kernel, out_shape=(jax.ShapeDtypeStruct(table.shape...]
    pallas_call x3 -> x4, Pallas kernels: 4.82 us -> 5.65 us  [the longest x2 2.49 us: scattered(): pl.pallas_call(kernel, out_shape=pltpu.VMEM((rows, blocks.shape[2]), jnp....]
  transfers between devices with their start and end apart: 5 -> 5, of which waited for: 2 -> 2; matrix products, arithmetic and copies ran while one was open for 0% -> 0% of each run, Pallas kernels for 13% -> 15%
where the time goes in v3:
time: 82.2 us; the launch traced here: 80.8 us
  waiting for transfers between devices  25.4 us (31%)
  blocking collectives  22.4 us (27%)
  Pallas kernels  21.5 us (26%)
  starting transfers between devices  10.6 us (13%)
    ppermute x1, waiting for transfers between devices, on_device(): far = lax.ppermute(near, 'zh', SWAP)  23.5 us
    all_to_all x1, blocking collectives, on_device(): own = lax.all_to_all(message, DEV, 0, 0, tiled=True)  22.4 us
    pallas_call x1, Pallas kernels, theirs_of(): pl.pallas_call(theirs_kernel, out_shape=(pltpu.VMEM(hidden.shape, jnp.bfl...  8.41 us
    all_to_all x1, starting transfers between devices, to_owners(): return lax.all_to_all(blocks, CHIPS, 0, 0, tiled=True)  7.2 us
    pallas_call x1, Pallas kernels, mine_of(): pl.pallas_call(mine_kernel, out_shape=pltpu.VMEM((2 * WIDTH, columns), jn...  3.43 us
    ppermute x1, starting transfers between devices, on_device(): far = lax.ppermute(near, 'zh', SWAP)  3.26 us
    pallas_call x1, Pallas kernels, updated(): pl.pallas_call(update_kernel, out_shape=(jax.ShapeDtypeStruct(table.shape...  3.17 us
    pallas_call x2, Pallas kernels, scattered(): pl.pallas_call(kernel, out_shape=pltpu.VMEM((rows, blocks.shape[2]), jnp....  2.49 us
  transfers between devices with their start and end apart: 5, of which 2 were waited for; matrix products, arithmetic and copies ran while one was open for 0% of the time, Pallas kernels for 15%

profile of v3, /device:TPU:0, one launch (start us, length us, event | category | flops | bytes accessed | tf_op | source)
XLA Modules:
  0.0 80.8 jit_solution(2997948634593985917)
XLA Ops:
  0.6 8.4 %theirs_of.1 = (bf16[2048,1024]{1,0:T(8,128)(2,1)S(1)}, bf16[512,1536]{1,0:T(8,128)(2,1)S(1)}, bf16[2048,512]{1,0:T(8,128)(2,1)S(1)}, bf16[2,2048,512]{2,1,0:T(8,128)(2,1)S(1)}, bf16[2048,1024]{1,0:T(8,128)(2,1)S(1)}) custom-call(s32[1]{0:T(128)} %bitcast.core_ref, bf16[2048,512]{1,0:T(8,128)(2,1)} %grad.1, bf16[1024,512]{1,0:T(8,128)(2,1)} %weight.1, ...), custom_call_target="tpu_custom_call" | custom-call | flops 5400000000 | bytes 11534336 | tf_op jit(solution)/shard_map/theirs_of/pallas_call | solution.py:259
  9.1 0.1 collective-permute-start
  9.1 1.9 %pack_rows.1 = bf16[32,72,128]{2,1,0:T(8,128)(2,1)} custom-call(s32[32]{0:T(128)} %counts_from.1, s32[16,128]{1,0:T(8,128)} %bitcast.6, bf16[32,64,128]{2,1,0:T(8,128)(2,1)} %bitcast.5), custom_call_target="tpu_custom_call" | custom-call | flops 1000000 | bytes 1048576 | tf_op jit(solution)/shard_map/pack_rows/pallas_call | solution.py:67
  11.1 22.4 %all_to_all.10.blocks = bf16[32,72,128]{2,1,0:T(8,128)(2,1)S(1)} all-to-all(bf16[32,72,128]{2,1,0:T(8,128)(2,1)} %pack_rows.1), channel_id=1, replica_groups=mesh['zh'=2,'c'=2,'y'=4,'x'=4,'zl'=2] {'y','x','zl'}, dimensions={0} | all-to-all | bytes 1179648 | tf_op jit(solution)/shard_map/all_to_all | solution.py:366
  33.4 0.0 collective-permute-start.1
  33.4 3.4 %mine_of.1.mine = f32[512,1536]{1,0:T(8,128)S(1)} custom-call(s32[1]{0:T(128)} %bitcast.core_ref, bf16[2,2048,512]{2,1,0:T(8,128)(2,1)S(1)} %get-tuple-element.13.given_kept, bf16[2048,1024]{1,0:T(8,128)(2,1)S(1)} %get-tuple-element.14.d_hidden, bf16[2048,1024]{1,0:T(8,128)(2,1)S(1)} %get-tuple-element.15.hidden_kept, ...), custom_call_target="tpu_custom_call" | custom-call | flops 3200000000 | bytes 2097152 | tf_op jit(solution)/shard_map/mine_of/pallas_call | solution.py:285
  36.9 0.0 collective-permute-done.arrived
  36.9 1.3 %join_halves.1 = bf16[512,1536]{1,0:T(8,128)(2,1)} custom-call(f32[512,1536]{1,0:T(8,128)S(1)} %mine_of.1.mine, bf16[512,1536]{1,0:T(8,128)(2,1)S(1)} %collective-permute-done.arrived), custom_call_target="tpu_custom_call" | custom-call | flops 1000000 | bytes 2097152 | tf_op jit(solution)/shard_map/join_halves/pallas_call | solution.py:310
  38.1 7.2 %all-to-all-start = ((bf16[64,8,1536]{2,1,0:T(8,128)(2,1)}), bf16[64,8,1536]{2,1,0:T(8,128)(2,1)S(1)}, u32[]{:S(2)}, u32[]{:S(2)}) async-start(bf16[64,8,1536]{2,1,0:T(8,128)(2,1)} %bitcast.4), calls=%async_computation | async-start | bytes 3145728 | tf_op jit(solution)/shard_map/all_to_all | solution.py:350
  45.4 1.2 %shard_map.120.acc = f32[1024,128]{1,0:T(8,128)S(1)} custom-call(s32[1]{0:T(128)} %bitcast.core_ref, bf16[32,72,128]{2,1,0:T(8,128)(2,1)S(1)} %all_to_all.10.blocks), custom_call_target="tpu_custom_call" | custom-call | flops 500000000 | bytes 1048576 | tf_op jit(solution)/shard_map/pallas_call | solution.py:116
  46.6 0.0 collective-permute-done.1.blocks
  46.6 1.2 %shard_map.121 = f32[1024,128]{1,0:T(8,128)S(1)} custom-call(s32[1]{0:T(128)} %bitcast.core_ref, bf16[32,72,128]{2,1,0:T(8,128)(2,1)S(1)} %collective-permute-done.1.blocks, f32[1024,128]{1,0:T(8,128)S(1)} %shard_map.120.acc), custom_call_target="tpu_custom_call" | custom-call | flops 500000000 | bytes 1048576 | tf_op jit(solution)/shard_map/pallas_call | solution.py:116
  47.9 3.3 %collective-permute-start.2 = (f16[1024,128]{1,0:T(8,128)(2,1)S(1)}, f16[1024,128]{1,0:T(8,128)(2,1)S(1)}, u32[]{:S(2)}, u32[]{:S(2)}) collective-permute-start(f16[1024,128]{1,0:T(8,128)(2,1)S(1)} %convert_element_type.9), channel_id=1, source_target_pairs={{0,64},{64,0},{1,65},{65,1},{2,66},{66,2},{3,67},{67,3},{4,68},{68... | collective-permute-start | bytes 786440 | tf_op jit(solution)/shard_map/ppermute | solution.py:382
  51.2 23.5 %collective-permute-done.2 = f16[1024,128]{1,0:T(8,128)(2,1)S(1)} collective-permute-done((f16[1024,128]{1,0:T(8,128)(2,1)S(1)}, f16[1024,128]{1,0:T(8,128)(2,1)S(1)}, u32[]{:S(2)}, u32[]{:S(2)}) %collective-permute-start.2) | collective-permute-done | bytes 262176 | tf_op jit(solution)/shard_map/ppermute | solution.py:382
  74.7 0.1 convert_add_fusion.total
  74.8 0.1 collective-permute-start.3
  74.8 1.9 %collective-permute-done.3.total_other = f32[1024,128]{1,0:T(8,128)S(1)} collective-permute-done((f32[1024,128]{1,0:T(8,128)S(1)}, f32[1024,128]{1,0:T(8,128)S(1)}, u32[]{:S(2)}, u32[]{:S(2)}) %collective-permute-start.3) | collective-permute-done | bytes 524320 | tf_op jit(solution)/shard_map/ppermute | solution.py:384
  76.7 3.2 %update_rows.1 = (f32[2048,128]{1,0:T(8,128)}, f32[2048,128]{1,0:T(8,128)}) custom-call(s32[1]{0:T(128)} %bitcast.core_ref, f32[1024,128]{1,0:T(8,128)S(1)} %convert_add_fusion.total, f32[1024,128]{1,0:T(8,128)S(1)} %collective-permute-done.3.total_other, f32[2048,128]{1,0:T(8,128)} %table.1, f32[2048,128]{1,0:T(8,128)} %state.1), custom_call_target="tpu_custom_call" | custom-call | flops 2000000 | bytes 5242880 | tf_op jit(solution)/shard_map/update_rows/pallas_call | solution.py:151
  79.9 0.0 all-to-all-done.blocks
  79.9 0.9 %total_blocks.1 = (f32[8,1024]{1,0:T(8,128)}, f32[8,512]{1,0:T(8,128)}) custom-call(bf16[64,8,1536]{2,1,0:T(8,128)(2,1)S(1)} %all-to-all-done.blocks), custom_call_target="tpu_custom_call" | custom-call | flops 1000000 | bytes 2097152 | tf_op jit(solution)/shard_map/total_blocks/pallas_call | solution.py:333
  (1 shorter events, 0.0 us)
Async XLA Ops:
  9.1 27.8 %collective-permute-start = (bf16[512,1536]{1,0:T(8,128)(2,1)S(1)}, bf16[512,1536]{1,0:T(8,128)(2,1)S(1)}, u32[]{:S(2)}, u32[]{:S(2)}) collective-permute-start(bf16[512,1536]{1,0:T(8,128)(2,1)S(1)} %get-tuple-element.17), channel_id=1, source_target_pairs={{0,32},{32,0},{1,33},{33,1},{2,34},{34,2},{3,35},{35,3},{4,36},{36... | collective-permute-start | bytes 4718600 | tf_op jit(solution)/shard_map/ppermute | solution.py:371
  33.4 13.2 %collective-permute-start.1 = (bf16[32,72,128]{2,1,0:T(8,128)(2,1)S(1)}, bf16[32,72,128]{2,1,0:T(8,128)(2,1)S(1)}, u32[]{:S(2)}, u32[]{:S(2)}) collective-permute-start(bf16[32,72,128]{2,1,0:T(8,128)(2,1)S(1)} %all_to_all.10.blocks), channel_id=1, source_target_pairs={{0,32},{32,0},{1,33},{33,1},{2,34},{34,2},{3,35},{35,3},{4,36},{36... | collective-permute-start | bytes 1769480 | tf_op jit(solution)/shard_map/ppermute | solution.py:377
  38.1 41.8 %all-to-all-start = ((bf16[64,8,1536]{2,1,0:T(8,128)(2,1)}), bf16[64,8,1536]{2,1,0:T(8,128)(2,1)S(1)}, u32[]{:S(2)}, u32[]{:S(2)}) async-start(bf16[64,8,1536]{2,1,0:T(8,128)(2,1)} %bitcast.4), calls=%async_computation | async-start | bytes 3145728 | tf_op jit(solution)/shard_map/all_to_all | solution.py:350
  47.9 26.8 %collective-permute-start.2 = (f16[1024,128]{1,0:T(8,128)(2,1)S(1)}, f16[1024,128]{1,0:T(8,128)(2,1)S(1)}, u32[]{:S(2)}, u32[]{:S(2)}) collective-permute-start(f16[1024,128]{1,0:T(8,128)(2,1)S(1)} %convert_element_type.9), channel_id=1, source_target_pairs={{0,64},{64,0},{1,65},{65,1},{2,66},{66,2},{3,67},{67,3},{4,68},{68... | collective-permute-start | bytes 786440 | tf_op jit(solution)/shard_map/ppermute | solution.py:382
  74.8 2.0 %collective-permute-start.3 = (f32[1024,128]{1,0:T(8,128)S(1)}, f32[1024,128]{1,0:T(8,128)S(1)}, u32[]{:S(2)}, u32[]{:S(2)}) collective-permute-start(f32[1024,128]{1,0:T(8,128)S(1)} %convert_add_fusion.total), channel_id=1, source_target_pairs={{0,32},{32,0},{1,33},{33,1},{2,34},{34,2},{3,35},{35,3},{4,36},{36... | collective-permute-start | bytes 1572872 | tf_op jit(solution)/shard_map/ppermute | solution.py:384
